TPU v7x, 512 devices: a whole 4x4x16 slice. The times are simulated.
512 devices in a mesh: req: 128 (over x_lo, z, y), tp: 4 (over x_hi, core).
Axes of the slice: x: 4 (x_hi: 2, x_lo: 2; x = x_hi * 2 + x_lo), y: 4, z: 16, core: 2. Of those that a mesh axis runs over, the one named last changes fastest.
Arguments:
- q_pre: bfloat16 [65536, 1024], P(('req', 'tp')), may hold values from -6 to 6
- gate_pre: bfloat16 [65536, 8], P(('req', 'tp')), may hold values from -6 to 6
- k_pre: bfloat16 [65536, 512], P(('req', 'tp')), may hold values from -6 to 6
- v_pre: bfloat16 [65536, 512], P(('req', 'tp')), may hold values from -6 to 6
- q_gain: float32 [128], replicated, may hold values from 0.1 to 1.9
- k_gain: float32 [128], replicated, may hold values from 0.1 to 1.9
- lengths: int32 [128, 3], P('req'), may hold values from 1 to 256, 512 in all within a row
- q_new: bfloat16 [384, 1024], P('req'), may hold values from -6 to 6
- gate_new: bfloat16 [384, 8], P('req'), may hold values from -6 to 6
- k_new: bfloat16 [384, 512], P('req'), may hold values from -6 to 6
- v_new: bfloat16 [384, 512], P('req'), may hold values from -6 to 6
- resid: bfloat16 [384, 2048], P('req'), may hold values from -5 to 5
- w_out: bfloat16 [1024, 2048], P('tp'), may hold values from -0.1875 to 0.1875
- norm_gain: float32 [2048], replicated, may hold values from 0.1 to 1.9
- w_gate: bfloat16 [2048, 3072], P('req', 'tp'), may hold values from -0.125 to 0.125
- w_up: bfloat16 [2048, 3072], P('req', 'tp'), may hold values from -0.125 to 0.125
- w_down: bfloat16 [3072, 2048], P('tp', 'req'), may hold values from -0.109375 to 0.109375
Outputs:
- prefill_out: bfloat16 [65536, 1024], P(('req', 'tp'))
- decode_out: bfloat16 [384, 2048], P('req')
Inputs may be any that keep to these rules, and one draw needn't show every extreme that they name: Each row holds the prompt lengths of one group's 3 requests; they sum to 512 and the longest is exactly 256.
All inputs are finite; a program needn't handle non-finite values.
Results may differ from a plain program's by a relative error of at most 0.0065.
Values may be sent and summed in bfloat16 or wider, within the bound.
A program may use at most 64 MiB of HBM per device.

v0:
```python
import jax
import jax.numpy as jnp
from jax import lax
from jax.sharding import PartitionSpec as P

rope_base = 1000000.0
norm_eps = 1e-06


def group_layout(lengths_row, total):
    req_ends = jnp.cumsum(lengths_row)
    req_starts = req_ends - lengths_row
    indices = jnp.arange(total, dtype=jnp.int32)
    segment = jnp.sum((indices[:, None] >= req_ends[None, :]).astype(jnp.int32), axis=1)
    onehot = segment[:, None] == jnp.arange(lengths_row.shape[0], dtype=jnp.int32)[None, :]
    offsets = jnp.sum(jnp.where(onehot, req_starts[None, :], 0), axis=1)
    return (segment, indices - offsets)


def head_norm(values, gain):
    mean_sq = jnp.mean(values * values, axis=-1, keepdims=True)
    return values * lax.rsqrt(mean_sq + norm_eps) * gain


def rotate(values, position):
    half_size = values.shape[-1] // 2
    freqs = rope_base ** (-(jnp.arange(half_size, dtype=jnp.float32) * 2.0 / (2 * half_size)))
    angles = position.astype(jnp.float32)[:, None] * freqs[None, :]
    shaped = (values.shape[0],) + (1,) * (values.ndim - 2) + (half_size,)
    cosine = jnp.cos(angles).reshape(shaped)
    sine = jnp.sin(angles).reshape(shaped)
    first_half = values[..., :half_size]
    second_half = values[..., half_size:]
    return jnp.concatenate(
        [first_half * cosine - second_half * sine, second_half * cosine + first_half * sine],
        axis=-1,
    )


def local(
    q_pre,
    gate_pre,
    k_pre,
    v_pre,
    q_gain,
    k_gain,
    lengths,
    q_new,
    gate_new,
    k_new,
    v_new,
    resid,
    w_out,
    norm_gain,
    w_gate,
    w_up,
    w_down,
):
    tok_rows = q_pre.shape[0]
    tp_count = lax.axis_size("tp")
    tp_index = lax.axis_index("tp")
    head_size = q_gain.shape[0]
    query_heads = gate_pre.shape[1]
    kv_heads = k_pre.shape[1] // head_size
    groups_per = query_heads // kv_heads
    kv_local = kv_heads // tp_count
    req_count = lengths.shape[1]
    score_scale = head_size ** (-0.5)
    segment, position = group_layout(lengths[0], tok_rows * tp_count)
    row_offset = tp_index * tok_rows
    seg_local = lax.dynamic_slice_in_dim(segment, row_offset, tok_rows)
    pos_local = lax.dynamic_slice_in_dim(position, row_offset, tok_rows)
    query_index = row_offset + jnp.arange(tok_rows, dtype=jnp.int32)
    queries = rotate(
        head_norm(q_pre.reshape(tok_rows, query_heads, head_size).astype(jnp.float32), q_gain),
        pos_local,
    )
    queries = queries.astype(jnp.bfloat16).reshape(tok_rows, kv_heads, groups_per, head_size)
    keys = rotate(
        head_norm(k_pre.reshape(tok_rows, kv_heads, head_size).astype(jnp.float32), k_gain),
        pos_local,
    ).astype(jnp.bfloat16)
    values = v_pre.reshape(tok_rows, kv_heads, head_size)

    def key_block(running, key_piece, value_piece, first_row):
        key_count = key_piece.shape[0]
        key_index = first_row + jnp.arange(key_count, dtype=jnp.int32)
        allowed = (seg_local[:, None] == segment[None, :]) & (
            query_index[:, None] >= key_index[None, :]
        )
        scores = (
            jnp.einsum(
                "qkgd,pkd->qkgp",
                queries,
                key_piece.reshape(key_count, kv_heads, head_size),
                preferred_element_type=jnp.float32,
            )
            * score_scale
        )
        weights = jnp.where(allowed[:, None, None, :], jnp.exp(scores), 0.0)
        totals = running[0] + jnp.sum(weights, axis=-1)
        mixed = running[1] + jnp.einsum(
            "qkgp,pkd->qkgd",
            weights.astype(jnp.bfloat16),
            value_piece.reshape(key_count, kv_heads, head_size),
            preferred_element_type=jnp.float32,
        )
        return (totals, mixed)

    start_state = (
        jnp.zeros((tok_rows, kv_heads, groups_per), jnp.float32),
        jnp.zeros((tok_rows, kv_heads, groups_per, head_size), jnp.float32),
    )
    pieces = (
        lax.all_gather(keys.reshape(tok_rows, kv_heads * head_size), "tp", axis=0, tiled=True),
        lax.all_gather(v_pre, "tp", axis=0, tiled=True),
    )
    key_count = pieces[0].shape[0]
    block_rows = 512

    def one_block(number, carried):
        begin_at = number * block_rows
        return key_block(carried, pieces[0], pieces[1], begin_at)

    totals, mixed = lax.fori_loop(0, key_count // block_rows, one_block, start_state)
    gates = jax.nn.sigmoid(gate_pre.astype(jnp.float32)).reshape(tok_rows, kv_heads, groups_per)
    prefill_out = (
        (mixed / totals[..., None] * gates[..., None])
        .astype(jnp.bfloat16)
        .reshape(tok_rows, query_heads * head_size)
    )
    new_queries = rotate(
        head_norm(q_new.reshape(req_count, query_heads, head_size).astype(jnp.float32), q_gain),
        lengths[0],
    )
    new_queries = new_queries.astype(jnp.bfloat16).reshape(
        req_count, kv_heads, groups_per, head_size
    )
    new_keys = rotate(
        head_norm(k_new.reshape(req_count, kv_heads, head_size).astype(jnp.float32), k_gain),
        lengths[0],
    ).astype(jnp.bfloat16)
    new_values = v_new.reshape(req_count, kv_heads, head_size)
    new_gates = jax.nn.sigmoid(gate_new.astype(jnp.float32)).reshape(
        req_count, kv_heads, groups_per
    )
    head_first = tp_index * kv_local
    request_ids = jnp.arange(req_count, dtype=jnp.int32)
    own_queries = lax.dynamic_slice_in_dim(new_queries, head_first, kv_local, 1)
    cache_keys, cache_values = (
        lax.all_to_all(keys, "tp", split_axis=1, concat_axis=0, tiled=True),
        lax.all_to_all(values, "tp", split_axis=1, concat_axis=0, tiled=True),
    )
    scores = (
        jnp.einsum("rkgd,pkd->rkgp", own_queries, cache_keys, preferred_element_type=jnp.float32)
        * score_scale
    )
    owned = segment[None, :] == request_ids[:, None]
    weights = jnp.where(owned[:, None, None, :], jnp.exp(scores), 0.0)
    weighted = jnp.einsum(
        "rkgp,pkd->rkgd",
        weights.astype(jnp.bfloat16),
        cache_values,
        preferred_element_type=jnp.float32,
    )
    dec_totals = jnp.sum(weights, axis=-1)
    dec_mixed = weighted
    own_keys = lax.dynamic_slice_in_dim(new_keys, head_first, kv_local, 1)
    own_values = lax.dynamic_slice_in_dim(new_values, head_first, kv_local, 1)
    own_gates = lax.dynamic_slice_in_dim(new_gates, head_first, kv_local, 1)
    self_weight = jnp.exp(
        jnp.einsum("rkgd,rkd->rkg", own_queries, own_keys, preferred_element_type=jnp.float32)
        * score_scale
    )
    dec_totals = dec_totals + self_weight
    dec_mixed = dec_mixed + self_weight[..., None] * own_values.astype(jnp.float32)[:, :, None, :]
    attended = (
        (dec_mixed / dec_totals[..., None] * own_gates[..., None])
        .astype(jnp.bfloat16)
        .reshape(req_count, kv_local * groups_per * head_size)
    )
    partial_out = jnp.dot(attended, w_out, preferred_element_type=jnp.float32)
    attn_rows = lax.psum(partial_out, "tp")
    hidden_state = resid.astype(jnp.float32) + attn_rows
    mean_sq = jnp.mean(hidden_state * hidden_state, axis=-1, keepdims=True)
    normed = (hidden_state * lax.rsqrt(mean_sq + norm_eps) * norm_gain).astype(jnp.bfloat16)
    units_local = w_gate.shape[1]
    paired = jnp.concatenate([w_gate, w_up], axis=1)
    columns = lax.all_to_all(normed, "req", split_axis=1, concat_axis=0, tiled=True)
    whole_sums = lax.psum(jnp.dot(columns, paired, preferred_element_type=jnp.float32), "req")
    hidden_units = (jax.nn.silu(whole_sums[:, :units_local]) * whole_sums[:, units_local:]).astype(
        jnp.bfloat16
    )
    down_part = jnp.dot(hidden_units, w_down, preferred_element_type=jnp.float32)
    back_part = lax.all_to_all(down_part, "req", split_axis=0, concat_axis=1, tiled=True)
    mlp_rows = lax.psum(back_part, "tp")
    decode_out = (hidden_state + mlp_rows).astype(jnp.bfloat16)
    return (prefill_out, decode_out)


def solution(mesh):
    return jax.shard_map(
        local,
        mesh=mesh,
        in_specs=(
            P(("req", "tp"), None),
            P(("req", "tp"), None),
            P(("req", "tp"), None),
            P(("req", "tp"), None),
            P(),
            P(),
            P("req", None),
            P("req", None),
            P("req", None),
            P("req", None),
            P("req", None),
            P("req", None),
            P("tp", None),
            P(),
            P("req", "tp"),
            P("req", "tp"),
            P("tp", "req"),
        ),
        out_specs=(P(("req", "tp"), None), P("req", None)),
        check_vma=False,
    )
```

profile of v0, /device:TPU:1, one launch (start us, length us, event | category | flops | bytes accessed | tf_op | source)
XLA Modules:
  0.0 1281.9 jit_solution(9922878994824692450)
XLA Ops:
  7.2 0.0 copy-start
  7.3 1.0 reduce-window.4
  8.2 0.7 convert_bitcast_fusion.2
  9.0 0.1 convert_reduce_fusion
  9.1 0.1 select_reduce_fusion
  9.1 1.0 copy.88
  10.2 0.1 dynamic-slice_convert_fusion
  10.3 0.2 multiply_cosine_fusion
  10.5 0.7 multiply_multiply_fusion.1
  11.3 0.7 maximum_convert_fusion
  12.0 10.2 all-to-all-start
  22.2 0.1 multiply_cosine_fusion.1
  22.3 0.1 fusion.30
  22.4 0.1 fusion.31
  22.5 0.1 subtract_convert_fusion.1
  22.6 0.1 multiply_reduce_fusion.3
  22.7 0.1 copy.102
  22.8 0.1 fusion.32
  22.9 0.1 subtract_convert_fusion.2
  23.0 0.1 fusion.43
  23.0 0.1 fusion.52
  23.1 0.1 fusion.44
  23.2 0.1 copy.115
  23.3 0.1 copy.105
  23.4 0.7 fusion.48
  24.1 0.7 copy_bitcast_fusion
  24.8 2.5 all-to-all-done
  27.3 4.3 all-to-all-start.1
  31.6 0.1 copy.98
  31.7 0.2 fusion.60
  32.0 4.7 all-to-all-done.1
  36.7 0.4 fusion.20
  37.0 13.5 %psum.21 = f32[3,2048]{1,0:T(4,128)S(1)} all-reduce(f32[3,2048]{1,0:T(4,128)S(1)} %fusion.20), channel_id=1, replica_groups=mesh['req'=128,'tp'=4] {'tp'}, use_global_device_ids=true, to_apply=%region_9.10 | all-reduce | flops 6144 | bytes 49152 | tf_op jit(solution)/shard_map/psum | solution.py:183
  50.6 0.1 multiply_reduce_fusion.2
  50.7 0.1 multiply_convert_fusion
  50.8 0.1 all_to_all.56
  50.9 0.1 copy.106
  51.0 30.8 %all_to_all.68 = bf16[3,128,16]{2,0,1:T(4,128)(2,1)S(1)} all-to-all(bf16[3,128,16]{2,0,1:T(4,128)(2,1)S(1)} %copy.106), channel_id=1, replica_groups=mesh['req'=128,'tp'=4] {'req'}, dimensions={1} | all-to-all | bytes 24576 | tf_op jit(solution)/shard_map/all_to_all | solution.py:189
  81.8 0.1 all_to_all.59
  81.9 1.8 fusion.26
  83.7 0.0 all-reduce.2.cloned.1.call-update
  83.7 0.1 copy.91
  83.8 0.1 copy.92
  83.9 0.1 dynamic_slice.18
  84.1 0.1 copy.120
  84.2 0.2 multiply_reduce_fusion
  84.4 0.1 copy.90
  84.6 0.2 multiply_multiply_fusion
  84.8 0.3 subtract_convert_fusion
  85.2 11.5 all_gather.7
  96.7 0.2 copy.96
  97.0 9.0 all_gather.6
  106.0 0.1 fusion.25
  106.2 2.0 fusion
  108.2 1051.9 %all-reduce.2.cloned.1.call-done = f32[384,1536]{1,0:T(8,128)} async-done(((f32[384,1536]{1,0:T(8,128)}), f32[384,1536]{1,0:T(8,128)}) %all-reduce.2.cloned.1.call-update) | async-done | bytes 2359312 | tf_op jit(solution)/shard_map/psum | solution.py:190
  1160.0 2.1 fusion.18
  1162.1 0.8 all_to_all.60
  1162.9 6.2 all-to-all-start.3
  1169.1 2.1 fusion.4
  1171.1 0.9 copy.109
  1172.0 15.7 %all-to-all-done.3 = f32[128,3,16]{2,1,0:T(4,128)S(1)} async-done(((f32[128,3,16]{2,1,0:T(4,128)}), f32[128,3,16]{2,1,0:T(4,128)S(1)}, u32[]{:S(2)}, u32[]{:S(2)}) %all-to-all-start.3) | async-done | bytes 24608 | tf_op jit(solution)/shard_map/all_to_all | solution.py:195
  1187.8 0.1 all_to_all.63
  1187.9 86.6 %psum.23 = f32[3,2048]{1,0:T(4,128)S(1)} all-reduce(f32[3,2048]{1,0:T(4,128)S(1)} %all_to_all.63), channel_id=1, replica_groups=mesh['req'=128,'tp'=4] {'tp'}, use_global_device_ids=true, to_apply=%region_12.13 | all-reduce | flops 6144 | bytes 49152 | tf_op jit(solution)/shard_map/psum | solution.py:196
  1274.5 0.6 add_convert_fusion.1
  (52 shorter events, 0.5 us)
Async XLA Ops:
  7.2 29.5 %copy-start = (bf16[256,2048]{1,0:T(8,128)(2,1)S(1)}, bf16[256,2048]{1,0:T(8,128)(2,1)}, u32[]{:S(2)}) copy-start(bf16[256,2048]{1,0:T(8,128)(2,1)} %param.29) | copy-start | bytes 3145732
  7.2 15.6 %copy-start.11 = (f32[128]{0:T(128)S(1)}, f32[128]{0:T(128)}, u32[]{:S(2)}) copy-start(f32[128]{0:T(128)} %param.22) | copy-start | bytes 1540
  7.2 15.1 %copy-start.7 = (bf16[3,1024]{1,0:T(4,128)(2,1)S(1)}, bf16[3,1024]{1,0:T(4,128)(2,1)}, u32[]{:S(2)}) copy-start(bf16[3,1024]{1,0:T(4,128)(2,1)} %param.24) | copy-start | bytes 18436
  7.2 15.2 %copy-start.9 = (f32[128]{0:T(128)S(1)}, f32[128]{0:T(128)}, u32[]{:S(2)}) copy-start(f32[128]{0:T(128)} %param.21) | copy-start | bytes 1540
  7.2 15.4 %copy-start.6 = (bf16[3,512]{1,0:T(4,128)(2,1)S(1)}, bf16[3,512]{1,0:T(4,128)(2,1)}, u32[]{:S(2)}) copy-start(bf16[3,512]{1,0:T(4,128)(2,1)} %param.26) | copy-start | bytes 9220
  7.2 16.1 %copy-start.12 = (bf16[3,8]{1,0:T(4,128)(2,1)S(1)}, bf16[3,8]{1,0:T(4,128)(2,1)}, u32[]{:S(2)}) copy-start(bf16[3,8]{1,0:T(4,128)(2,1)} %param.25) | copy-start | bytes 148
  7.2 16.9 %copy-start.1 = (bf16[128,512]{1,0:T(8,128)(2,1)S(1)}, bf16[128,512]{1,0:T(8,128)(2,1)}, u32[]{:S(2)}) copy-start(bf16[128,512]{1,0:T(8,128)(2,1)} %param.20) | copy-start | bytes 393220
  10.2 40.4 %copy-start.3 = (bf16[3,2048]{1,0:T(4,128)(2,1)S(1)}, bf16[3,2048]{1,0:T(4,128)(2,1)}, u32[]{:S(2)}) copy-start(bf16[3,2048]{1,0:T(4,128)(2,1)} %param.28) | copy-start | bytes 36868
  10.3 40.4 %copy-start.8 = (f32[2048]{0:T(1024)S(1)}, f32[2048]{0:T(1024)}, u32[]{:S(2)}) copy-start(f32[2048]{0:T(1024)} %param.30) | copy-start | bytes 24580
  11.3 70.6 %copy-start.4 = (bf16[16,768]{1,0:T(8,128)(2,1)S(1)}, bf16[16,768]{1,0:T(8,128)(2,1)}, u32[]{:S(2)}) copy-start(bf16[16,768]{1,0:T(8,128)(2,1)} %param.32) | copy-start | bytes 73732
  11.3 70.6 %copy-start.5 = (bf16[16,768]{1,0:T(8,128)(2,1)S(1)}, bf16[16,768]{1,0:T(8,128)(2,1)}, u32[]{:S(2)}) copy-start(bf16[16,768]{1,0:T(8,128)(2,1)} %param.31) | copy-start | bytes 73732
  12.0 15.3 %all-to-all-start = ((bf16[128,4,128]{0,2,1:T(8,128)(2,1)}), bf16[128,4,128]{0,2,1:T(8,128)(2,1)S(1)}, u32[]{:S(2)}, u32[]{:S(2)}) async-start(bf16[128,4,128]{0,2,1:T(8,128)(2,1)} %maximum_convert_fusion), calls=%async_computation | async-start | bytes 262144 | tf_op jit(solution)/shard_map/all_to_all | solution.py:151
  27.3 9.4 all-to-all-start.1
  31.6 1128.4 %all-reduce.2.cloned.1.call-start = ((), (), s32[]{:S(2)}) async-start(), calls=%async_computation.4 | async-start | bytes 4718592 | tf_op jit(solution)/shard_map/psum | solution.py:190
  81.9 2.1 copy-start.2
  85.1 20.9 %copy-start.10 = (bf16[128,8]{0,1:T(8,128)(2,1)S(1)}, bf16[128,8]{0,1:T(8,128)(2,1)}, u32[]{:S(2)}) copy-start(bf16[128,8]{0,1:T(8,128)(2,1)} %param.18) | copy-start | bytes 6148
  96.9 1063.1 %copy-start.13 = (bf16[768,16]{0,1:T(8,128)(2,1)S(1)}, bf16[768,16]{0,1:T(8,128)(2,1)}, u32[]{:S(2)}) copy-start(bf16[768,16]{0,1:T(8,128)(2,1)} %param.33) | copy-start | bytes 73732
  1162.9 24.9 %all-to-all-start.3 = ((f32[128,3,16]{2,1,0:T(4,128)}), f32[128,3,16]{2,1,0:T(4,128)S(1)}, u32[]{:S(2)}, u32[]{:S(2)}) async-start(f32[128,3,16]{2,1,0:T(4,128)} %all_to_all.60), calls=%async_computation.3 | async-start | bytes 524288 | tf_op jit(solution)/shard_map/all_to_all | solution.py:195
Sparse Core Ops, SparseCore 0:
  83.9 1076.1 all-reduce.1
where the time goes:
time: 1280 us
  waiting for transfers between devices  1070 us (84%)
  blocking collectives  151 us (12%)
  starting transfers between devices  20.7 us (2%)
  between operations  14.4 us (1%)
    psum x1, waiting for transfers between devices, local(): lax.psum(jnp.dot(columns, paired, preferred_element_type=jnp.float32), 'r...  1050 us
    psum x1, blocking collectives, local(): mlp_rows = lax.psum(back_part, 'tp')  86.6 us
    all_to_all x1, blocking collectives, local(): lax.all_to_all(normed, 'req', split_axis=1, concat_axis=0, tiled=True)  30.8 us
  transfers between devices with their start and end apart: 4, of which 4 were waited for; matrix products, arithmetic and copies ran while one was open for 1% of the time, Pallas kernels for 0%

commit v1 on v0

--- a/solution.py
+++ b/solution.py
@@ -5,6 +5,8 @@
 
 rope_base = 1000000.0
 norm_eps = 1e-06
+req = ("xlo", "z", "y")
+tp = ("xhi", "core")
 
 
 def group_layout(lengths_row, total):
@@ -57,8 +59,8 @@
     w_down,
 ):
     tok_rows = q_pre.shape[0]
-    tp_count = lax.axis_size("tp")
-    tp_index = lax.axis_index("tp")
+    tp_count = lax.axis_size(tp)
+    tp_index = lax.axis_index(tp)
     head_size = q_gain.shape[0]
     query_heads = gate_pre.shape[1]
     kv_heads = k_pre.shape[1] // head_size
@@ -112,8 +114,8 @@
         jnp.zeros((tok_rows, kv_heads, groups_per, head_size), jnp.float32),
     )
     pieces = (
-        lax.all_gather(keys.reshape(tok_rows, kv_heads * head_size), "tp", axis=0, tiled=True),
-        lax.all_gather(v_pre, "tp", axis=0, tiled=True),
+        lax.all_gather(keys.reshape(tok_rows, kv_heads * head_size), tp, axis=0, tiled=True),
+        lax.all_gather(v_pre, tp, axis=0, tiled=True),
     )
     key_count = pieces[0].shape[0]
     block_rows = 512
@@ -144,27 +146,26 @@
     new_gates = jax.nn.sigmoid(gate_new.astype(jnp.float32)).reshape(
         req_count, kv_heads, groups_per
     )
+    request_ids = jnp.arange(req_count, dtype=jnp.int32)
+    dec_scores = (
+        jnp.einsum("rkgd,pkd->rkgp", new_queries, keys, preferred_element_type=jnp.float32)
+        * score_scale
+    )
+    owned = seg_local[None, :] == request_ids[:, None]
+    dec_weights = jnp.where(owned[:, None, None, :], jnp.exp(dec_scores), 0.0)
+    dec_part = jnp.einsum(
+        "rkgp,pkd->rkgd",
+        dec_weights.astype(jnp.bfloat16),
+        values,
+        preferred_element_type=jnp.float32,
+    )
+    dec_sum = jnp.sum(dec_weights, axis=-1, keepdims=True)
+    both = jnp.concatenate([dec_part, jnp.broadcast_to(dec_sum, dec_part.shape)], axis=0)
+    both = lax.psum(both, tp)
     head_first = tp_index * kv_local
-    request_ids = jnp.arange(req_count, dtype=jnp.int32)
+    both = lax.dynamic_slice_in_dim(both, head_first, kv_local, 1)
+    dec_mixed, dec_totals = both[:req_count], both[req_count:, ..., 0]
     own_queries = lax.dynamic_slice_in_dim(new_queries, head_first, kv_local, 1)
-    cache_keys, cache_values = (
-        lax.all_to_all(keys, "tp", split_axis=1, concat_axis=0, tiled=True),
-        lax.all_to_all(values, "tp", split_axis=1, concat_axis=0, tiled=True),
-    )
-    scores = (
-        jnp.einsum("rkgd,pkd->rkgp", own_queries, cache_keys, preferred_element_type=jnp.float32)
-        * score_scale
-    )
-    owned = segment[None, :] == request_ids[:, None]
-    weights = jnp.where(owned[:, None, None, :], jnp.exp(scores), 0.0)
-    weighted = jnp.einsum(
-        "rkgp,pkd->rkgd",
-        weights.astype(jnp.bfloat16),
-        cache_values,
-        preferred_element_type=jnp.float32,
-    )
-    dec_totals = jnp.sum(weights, axis=-1)
-    dec_mixed = weighted
     own_keys = lax.dynamic_slice_in_dim(new_keys, head_first, kv_local, 1)
     own_values = lax.dynamic_slice_in_dim(new_values, head_first, kv_local, 1)
     own_gates = lax.dynamic_slice_in_dim(new_gates, head_first, kv_local, 1)
@@ -180,47 +181,68 @@
         .reshape(req_count, kv_local * groups_per * head_size)
     )
     partial_out = jnp.dot(attended, w_out, preferred_element_type=jnp.float32)
-    attn_rows = lax.psum(partial_out, "tp")
+    attn_rows = lax.psum(partial_out, tp)
     hidden_state = resid.astype(jnp.float32) + attn_rows
     mean_sq = jnp.mean(hidden_state * hidden_state, axis=-1, keepdims=True)
     normed = (hidden_state * lax.rsqrt(mean_sq + norm_eps) * norm_gain).astype(jnp.bfloat16)
+    width = normed.shape[1]
+    rows_each = w_gate.shape[0]
+    nx, nz, ny = lax.axis_size("xlo"), lax.axis_size("z"), lax.axis_size("y")
+    stacked = jnp.concatenate([w_gate, w_up, w_down.T], axis=1)
+    gathered = lax.all_gather(stacked, "z", axis=0, tiled=True)
     units_local = w_gate.shape[1]
-    paired = jnp.concatenate([w_gate, w_up], axis=1)
-    columns = lax.all_to_all(normed, "req", split_axis=1, concat_axis=0, tiled=True)
-    whole_sums = lax.psum(jnp.dot(columns, paired, preferred_element_type=jnp.float32), "req")
-    hidden_units = (jax.nn.silu(whole_sums[:, :units_local]) * whole_sums[:, units_local:]).astype(
-        jnp.bfloat16
-    )
-    down_part = jnp.dot(hidden_units, w_down, preferred_element_type=jnp.float32)
-    back_part = lax.all_to_all(down_part, "req", split_axis=0, concat_axis=1, tiled=True)
-    mlp_rows = lax.psum(back_part, "tp")
+    plane = lax.all_gather(normed, ("xlo", "y"), axis=0, tiled=True)
+    plane = plane.reshape(-1, nx, nz, ny, rows_each)
+    plane = lax.dynamic_index_in_dim(plane, lax.axis_index("xlo"), 1, keepdims=False)
+    plane = lax.dynamic_index_in_dim(plane, lax.axis_index("y"), 2, keepdims=False)
+    columns = plane.reshape(plane.shape[0], nz * rows_each)
+    sums = lax.psum(
+        jnp.dot(columns, gathered[:, : 2 * units_local], preferred_element_type=jnp.float32),
+        ("xlo", "y"),
+    )
+    hidden_units = (jax.nn.silu(sums[:, :units_local]) * sums[:, units_local:]).astype(jnp.bfloat16)
+    down_part = lax.dot_general(
+        hidden_units,
+        gathered[:, 2 * units_local :],
+        (((1,), (1,)), ((), ())),
+        preferred_element_type=jnp.float32,
+    )
+    down_part = lax.psum(down_part, tp)
+    back = lax.all_gather(down_part, ("xlo", "y"), axis=0, tiled=False)
+    group = lax.axis_index(("xlo", "y"))
+    back = lax.dynamic_slice_in_dim(back, group * req_count, req_count, 1)
+    back = back.reshape(nx, ny, req_count, nz, rows_each).transpose(2, 0, 3, 1, 4)
+    mlp_rows = back.reshape(req_count, width)
     decode_out = (hidden_state + mlp_rows).astype(jnp.bfloat16)
     return (prefill_out, decode_out)
 
 
 def solution(mesh):
+    wide = jax.sharding.Mesh(
+        mesh.devices.reshape(2, 16, 4, 2, 2), ("xlo", "z", "y", "xhi", "core")
+    )
     return jax.shard_map(
         local,
-        mesh=mesh,
+        mesh=wide,
         in_specs=(
-            P(("req", "tp"), None),
-            P(("req", "tp"), None),
-            P(("req", "tp"), None),
-            P(("req", "tp"), None),
+            P(req + tp, None),
+            P(req + tp, None),
+            P(req + tp, None),
+            P(req + tp, None),
             P(),
             P(),
-            P("req", None),
-            P("req", None),
-            P("req", None),
-            P("req", None),
-            P("req", None),
-            P("req", None),
-            P("tp", None),
+            P(req, None),
+            P(req, None),
+            P(req, None),
+            P(req, None),
+            P(req, None),
+            P(req, None),
+            P(tp, None),
             P(),
-            P("req", "tp"),
-            P("req", "tp"),
-            P("tp", "req"),
+            P(req, tp),
+            P(req, tp),
+            P(tp, req),
         ),
-        out_specs=(P(("req", "tp"), None), P("req", None)),
+        out_specs=(P(req + tp, None), P(req, None)),
         check_vma=False,
     )

time: 1280 us -> 242 us (0.19)
  the two profiles are of different devices: /device:TPU:1 before, /device:TPU:4 now
where the time goes in v1:
time: 242 us; the launch traced here: 241 us
  blocking collectives  118 us (49%)
  waiting for transfers between devices  85 us (35%)
  between operations  14.4 us (6%)
  other arithmetic  9.47 us (4%)
  matrix products  8.14 us (3%)
  local copies, waits for them, and re-layouts  6.02 us (2%)
    psum x1, waiting for transfers between devices, local(): lax.psum(jnp.dot(columns, gathered[:, :2 * units_local], preferred_elemen...  84.9 us
    all_gather x1, blocking collectives, local(): back = lax.all_gather(down_part, ('xlo', 'y'), axis=0, tiled=False)  28.3 us
    all_gather x1, blocking collectives, local(): plane = lax.all_gather(normed, ('xlo', 'y'), axis=0, tiled=True)  28.2 us
    psum x1, blocking collectives, local(): attn_rows = lax.psum(partial_out, tp)  16.2 us
    psum x1, blocking collectives, local(): both = lax.psum(both, tp)  15.4 us
    psum x1, blocking collectives, local(): down_part = lax.psum(down_part, tp)  13.5 us
    all_gather x1, blocking collectives, local(): lax.all_gather(keys.reshape(tok_rows, kv_heads * head_size), tp, axis=0,...  8.81 us
    all_gather x1, blocking collectives, local(): lax.all_gather(v_pre, tp, axis=0, tiled=True)  8 us
  transfers between devices with their start and end apart: 2, of which 1 were waited for; matrix products, arithmetic and copies ran while one was open for 7% of the time, Pallas kernels for 0%

profile of v1, /device:TPU:4, one launch (start us, length us, event | category | flops | bytes accessed | tf_op | source)
XLA Modules:
  0.0 241.5 jit_solution(15434772363343229033)
XLA Ops:
  7.3 1.5 pad_maximum_fusion
  8.8 0.8 reduce-window.4
  9.7 0.7 convert_bitcast_fusion.2
  10.4 0.1 convert_reduce_fusion
  10.5 0.1 select_reduce_fusion
  10.7 0.1 dynamic-slice_convert_fusion
  10.7 1.0 copy.78
  11.8 0.1 copy.79
  12.0 0.3 multiply_cosine_fusion
  12.3 0.1 multiply_cosine_fusion.1
  12.4 0.7 convert_bitcast_fusion.1
  13.2 0.1 fusion.26
  13.3 0.7 fusion.27
  14.0 0.1 subtract_convert_fusion.1
  14.1 0.9 reshape.333
  15.0 0.8 multiply_multiply_fusion.1
  15.8 0.1 multiply_subtract_fusion
  16.0 0.1 maximum_convert_fusion
  16.1 0.2 fusion.7
  16.3 0.1 fusion.30
  16.4 0.2 convolution_bitcast_fusion.2
  16.6 15.4 %psum.28 = f32[6,4,2,128]{3,0,2,1:T(8,128)S(1)} all-reduce(f32[6,4,2,128]{3,0,2,1:T(8,128)S(1)} %pad_maximum_fusion.1), channel_id=1, replica_groups=mesh['xlo'=2,'z'=16,'y'=4,'xhi'=2,'core'=2] {'xhi','core'}, use_global_device_ids=true, to_apply=%region_8.9 | all-reduce | flops 6144 | bytes 49152 | tf_op jit(solution)/shard_map/psum | solution.py:164
  32.0 0.1 fusion.41
  32.1 0.1 multiply_reduce_fusion.3
  32.2 0.1 copy.91
  32.3 0.1 fusion.29
  32.4 0.1 subtract_convert_fusion.2
  32.4 0.1 fusion.50
  32.5 0.1 fusion.42
  32.6 0.1 copy.105
  32.7 0.1 copy.94
  32.9 0.7 fusion.46
  33.6 0.1 dynamic-slice_reduce_fusion.1
  33.7 0.3 fusion.36
  34.0 16.2 %psum.29 = f32[3,2048]{1,0:T(4,128)S(1)} all-reduce(f32[3,2048]{1,0:T(4,128)S(1)} %fusion.36), channel_id=1, replica_groups=mesh['xlo'=2,'z'=16,'y'=4,'xhi'=2,'core'=2] {'xhi','core'}, use_global_device_ids=true, to_apply=%region_10.11 | all-reduce | flops 6144 | bytes 49152 | tf_op jit(solution)/shard_map/psum | solution.py:184
  50.2 0.1 multiply_reduce_fusion.2
  50.3 0.1 fusion.25
  50.5 0.1 copy.80
  50.6 28.2 %all-gather = bf16[8,3,2048]{2,1,0:T(4,128)(2,1)S(1)} all-gather(bf16[1,3,2048]{2,1,0:T(4,128)(2,1)S(1)} %fusion.25), channel_id=1, replica_groups=mesh['xlo'=2,'z'=16,'y'=4,'xhi'=2,'core'=2] {'xlo','y'}, dimensions={0}, use_global_device_ids=true | all-gather | bytes 110592 | tf_op jit(solution)/shard_map/all_gather | solution.py:194
  78.8 0.6 reshape.339
  79.4 0.7 dynamic-slice_reduce_fusion
  80.1 0.1 reshape.340
  80.2 0.1 copy.110
  80.3 0.2 multiply_reduce_fusion
  80.6 0.1 copy.82
  80.7 0.2 multiply_multiply_fusion
  80.9 0.3 subtract_convert_fusion
  81.3 0.1 copy-done.1
  81.4 8.0 %all_gather.19 = bf16[512,512]{1,0:T(8,128)(2,1)S(1)} all-gather(bf16[128,512]{1,0:T(8,128)(2,1)S(1)} %copy-done.1), channel_id=1, replica_groups=mesh['xlo'=2,'z'=16,'y'=4,'xhi'=2,'core'=2] {'xhi','core'}, dimensions={0}, use_global_device_ids=true | all-gather | bytes 655360 | tf_op jit(solution)/shard_map/all_gather | solution.py:118
  89.4 0.2 copy.86
  89.7 8.8 %all_gather.18 = bf16[512,512]{0,1:T(8,128)(2,1)S(1)} all-gather(bf16[128,512]{0,1:T(8,128)(2,1)S(1)} %bitcast.114), channel_id=1, replica_groups=mesh['xlo'=2,'z'=16,'y'=4,'xhi'=2,'core'=2] {'xhi','core'}, dimensions={0}, use_global_device_ids=true | all-gather | bytes 655360 | tf_op jit(solution)/shard_map/all_gather | solution.py:117
  98.5 0.1 fusion.19
  98.6 2.0 fusion
  100.6 2.0 fusion.12
  102.7 2.1 fusion.4
  104.8 0.9 copy.97
  105.6 84.9 %all-reduce.2.cloned.1.call-done = f32[24,1536]{1,0:T(8,128)} async-done(((f32[24,1536]{1,0:T(8,128)}), f32[24,1536]{1,0:T(8,128)}) %all-reduce.2.cloned.1.call-update) | async-done | bytes 147472 | tf_op jit(solution)/shard_map/psum | solution.py:199
  190.5 1.3 convolution_bitcast_fusion.1
  191.8 13.5 %psum.31 = f32[1,24,256]{2,1,0:T(8,128)S(1)} all-reduce(f32[1,24,256]{2,1,0:T(8,128)S(1)} %convolution_bitcast_fusion.1), channel_id=1, replica_groups=mesh['xlo'=2,'z'=16,'y'=4,'xhi'=2,'core'=2] {'xhi','core'}, use_global_device_ids=true, to_apply=%region_13.14 | all-reduce | flops 6144 | bytes 49152 | tf_op jit(solution)/shard_map/psum | solution.py:210
  205.3 28.3 %all_gather.23 = f32[8,24,256]{2,1,0:T(8,128)S(1)} all-gather(f32[1,24,256]{2,1,0:T(8,128)S(1)} %psum.31), channel_id=1, replica_groups=mesh['xlo'=2,'z'=16,'y'=4,'xhi'=2,'core'=2] {'xlo','y'}, dimensions={0}, use_global_device_ids=true | all-gather | bytes 221184 | tf_op jit(solution)/shard_map/all_gather | solution.py:211
  233.6 0.1 reshape.341
  233.7 0.1 copy.96
  233.8 0.2 reshape.342
  234.0 0.6 add_convert_fusion.1
  (49 shorter events, 0.6 us)
Async XLA Ops:
  7.2 26.5 %copy-start = (bf16[256,2048]{1,0:T(8,128)(2,1)S(1)}, bf16[256,2048]{1,0:T(8,128)(2,1)}, u32[]{:S(2)}) copy-start(bf16[256,2048]{1,0:T(8,128)(2,1)} %param.29) | copy-start | bytes 3145732
  7.2 25.1 %copy-start.8 = (f32[128]{0:T(128)S(1)}, f32[128]{0:T(128)}, u32[]{:S(2)}) copy-start(f32[128]{0:T(128)} %param.22) | copy-start | bytes 1540
  7.2 24.9 %copy-start.4 = (bf16[3,512]{1,0:T(4,128)(2,1)S(1)}, bf16[3,512]{1,0:T(4,128)(2,1)}, u32[]{:S(2)}) copy-start(bf16[3,512]{1,0:T(4,128)(2,1)} %param.26) | copy-start | bytes 9220
  7.2 25.5 %copy-start.9 = (bf16[3,8]{1,0:T(4,128)(2,1)S(1)}, bf16[3,8]{1,0:T(4,128)(2,1)}, u32[]{:S(2)}) copy-start(bf16[3,8]{1,0:T(4,128)(2,1)} %param.25) | copy-start | bytes 148
  7.2 93.4 %all-gather.3.cloned.1.call-start = ((), (), s32[]{:S(2)}) async-start(), calls=%async_computation | async-start | bytes 1253376 | tf_op jit(solution)/shard_map/all_gather | solution.py:192
  8.8 181.8 %all-reduce.2.cloned.1.call-start = ((), (), s32[]{:S(2)}) async-start(), calls=%async_computation.1 | async-start | bytes 294912 | tf_op jit(solution)/shard_map/psum | solution.py:199
  12.0 38.2 %copy-start.3 = (bf16[3,2048]{1,0:T(4,128)(2,1)S(1)}, bf16[3,2048]{1,0:T(4,128)(2,1)}, u32[]{:S(2)}) copy-start(bf16[3,2048]{1,0:T(4,128)(2,1)} %param.28) | copy-start | bytes 36868
  12.3 38.1 %copy-start.5 = (f32[2048]{0:T(1024)S(1)}, f32[2048]{0:T(1024)}, u32[]{:S(2)}) copy-start(f32[2048]{0:T(1024)} %param.30) | copy-start | bytes 24580
  12.4 38.0 %copy-start.2 = (bf16[128,1024]{1,0:T(8,128)(2,1)S(1)}, bf16[128,1024]{1,0:T(8,128)(2,1)}, u32[]{:S(2)}) copy-start(bf16[128,1024]{1,0:T(8,128)(2,1)} %param.17) | copy-start | bytes 786436
  50.4 30.3 %copy-start.6 = (f32[128]{0:T(128)S(1)}, f32[128]{0:T(128)}, u32[]{:S(2)}) copy-start(f32[128]{0:T(128)} %param.21) | copy-start | bytes 1540
  80.5 0.9 copy-start.1
  81.2 17.2 %copy-start.7 = (bf16[128,8]{0,1:T(8,128)(2,1)S(1)}, bf16[128,8]{0,1:T(8,128)(2,1)}, u32[]{:S(2)}) copy-start(bf16[128,8]{0,1:T(8,128)(2,1)} %param.18) | copy-start | bytes 6148
Sparse Core Ops, SparseCore 0:
  10.7 76.0 all-gather.2
  102.8 87.7 all-reduce.1

commit v2 on v1

v2 whole, which is shorter than its diff:
```python
import functools

import jax
import jax.numpy as jnp
from jax import lax
from jax.experimental import pallas as pl
from jax.experimental.pallas import tpu as pltpu
from jax.sharding import PartitionSpec as P

rope_base = 1000000.0
norm_eps = 1e-06
req = ("xlo", "z", "y")
tp = ("xhi", "core")
NX, NZ, NY, NT = 2, 16, 4, 4
NP = NX * NY
HD = 128
HEADS = 8
KVH = 4
TOK = 128
CHUNK = 96
MASKED = -1e30
f32 = jnp.float32
bf16 = jnp.bfloat16


def iota(shape, dim):
    return lax.broadcasted_iota(jnp.int32, shape, dim)


def roll(values, shift, axis):
    return pltpu.roll(values, shift, axis)


def nt_dot(a, b):
    return lax.dot_general(a, b, (((1,), (1,)), ((), ())), preferred_element_type=f32)


def rope_tables(position):
    lane = iota(position.shape, 1)
    index = (lane % 64).astype(f32)
    freqs = jnp.exp(index * (-2.0 / HD * 13.815510557964274))
    angles = position * freqs
    sine = jnp.sin(angles)
    return jnp.cos(angles), jnp.where(lane < 64, -sine, sine)


def norm_rope(values, gain, cosine, sine):
    mean_sq = jnp.mean(values * values, axis=-1, keepdims=True)
    normed = values * lax.rsqrt(mean_sq + norm_eps) * gain
    return normed * cosine + roll(normed, 64, 1) * sine


def swap_halves(values):
    keep = (iota((8, 128), 0) < 4) == (iota((8, 128), 1) < 64)
    tiles = []
    for j in range(values.shape[1] // 128):
        tile = values[:, j * 128 : (j + 1) * 128]
        tiles.append(jnp.where(keep, tile, roll(roll(tile, 64, 1), 4, 0)))
    return jnp.concatenate(tiles, axis=1)


def kernel(
    lengths_ref,
    q_ref,
    gate_ref,
    k_ref,
    v_ref,
    qg_ref,
    kg_ref,
    qn_ref,
    gn_ref,
    kn_ref,
    vn_ref,
    resid_ref,
    wo_ref,
    ng_ref,
    wg_ref,
    wu_ref,
    wd_ref,
    out_ref,
    dec_ref,
    keys,
    vals,
    bias,
    nq,
    nk,
    nv,
    ngate,
    selfw,
    fold,
    piece_out,
    piece_in,
    gathered,
    x1_out,
    x1_in,
    x2,
    xa,
    xb_out,
    xb_in,
    xc,
    cos_t,
    sin_t,
    gates,
    s1_send,
    s1_recv,
    kv_send,
    kv_recv,
    x1_send,
    x1_recv,
    x2_send,
    x2_recv,
    xa_send,
    xa_recv,
    xb_send,
    xb_recv,
    xc_send,
    xc_recv,
    right_send,
    right_recv,
    left_send,
    left_recv,
):
    xlo, z, y = lax.axis_index("xlo"), lax.axis_index("z"), lax.axis_index("y")
    t = lax.axis_index("xhi") * 2 + lax.axis_index("core")
    p = xlo * NY + y

    def tp_dev(i):
        return {"xhi": i // 2, "core": i % 2}

    def plane_dev(i):
        return {"xlo": i // NY, "y": i % NY}

    def z_dev(i):
        return {"z": i % NZ}

    barrier = pltpu.get_barrier_semaphore()
    mesh_id = pl.DeviceIdType.MESH
    for d in range(1, NT):
        pl.semaphore_signal(barrier, inc=1, device_id=tp_dev((t + d) % NT), device_id_type=mesh_id)
    for d in range(1, NP):
        pl.semaphore_signal(barrier, inc=1, device_id=plane_dev((p + d) % NP), device_id_type=mesh_id)
    pl.semaphore_signal(barrier, inc=1, device_id=z_dev(z + 1), device_id_type=mesh_id)
    pl.semaphore_signal(barrier, inc=1, device_id=z_dev(z + NZ - 1), device_id_type=mesh_id)

    started = []

    def send(src, dst, send_sem, recv_sem, device):
        copy = pltpu.make_async_remote_copy(
            src_ref=src,
            dst_ref=dst,
            send_sem=send_sem,
            recv_sem=recv_sem,
            device_id=device,
            device_id_type=mesh_id,
        )
        copy.start()
        started.append(copy)
        return copy

    for n, ref in enumerate((wg_ref, wu_ref, wd_ref)):
        whole = ref[...].astype(f32)
        width = whole.shape[1]
        for i in range(NP):
            part = whole if i == 0 else roll(whole, width - CHUNK * i, 1)
            piece_out[i, :, n * 128 : (n + 1) * 128] = part[:, :128].astype(bf16)
    piece_in[pl.ds(p, 1)] = piece_out[pl.ds(p, 1)]

    pl.semaphore_wait(barrier, NT - 1 + NP - 1 + 2)
    s1 = [
        send(piece_out.at[(p + d) % NP], piece_in.at[p], s1_send.at[d - 1], s1_recv.at[d - 1], plane_dev((p + d) % NP))
        for d in range(1, NP)
    ]

    len0, len1, len2 = lengths_ref[0, 0], lengths_ref[0, 1], lengths_ref[0, 2]
    end0, end1 = len0, len0 + len1
    end2 = end1 + len2

    def start_of(index):
        return jnp.where(index >= end1, end1, jnp.where(index >= end0, end0, 0))

    own_index = t * TOK + iota((TOK, 128), 0)
    cosine, sine = rope_tables((own_index - start_of(own_index)).astype(f32))
    cos_t[...] = cosine
    sin_t[...] = sine

    k_gain = kg_ref[...]
    q_gain = qg_ref[...]
    for k in range(KVH):
        lanes = slice(k * HD, (k + 1) * HD)
        keys[2, :, lanes] = norm_rope(k_ref[:, lanes].astype(f32), k_gain, cosine, sine).astype(bf16)
    for d in (1, 2):

        @pl.when(t + d < NT)
        def _(d=d):
            for n, (src, dst) in enumerate(((keys.at[2], keys.at[2 - d]), (v_ref, vals.at[2 - d]))):
                pltpu.make_async_remote_copy(
                    src_ref=src,
                    dst_ref=dst,
                    send_sem=kv_send.at[d - 1, n],
                    recv_sem=kv_recv.at[d - 1, n],
                    device_id=tp_dev(lax.rem(t + d, NT)),
                    device_id_type=mesh_id,
                ).start()

        @pl.when(t < d)
        def _(d=d):
            keys[2 - d] = jnp.zeros((TOK, KVH * HD), bf16)
            vals[2 - d] = jnp.zeros((TOK, KVH * HD), bf16)

    for ref in (nq, nk, nv, ngate):
        ref[...] = jnp.zeros_like(ref)
    for h in range(HEADS):
        rows = slice(h * 4, h * 4 + 3)
        lanes = slice(h * HD, (h + 1) * HD)
        kv_lanes = slice(h // 2 * HD, (h // 2 + 1) * HD)
        nq[rows, :] = qn_ref[:, lanes].astype(f32)
        nk[rows, :] = kn_ref[:, kv_lanes].astype(f32)
        nv[rows, :] = vn_ref[:, kv_lanes].astype(f32)
        ngate[rows, :] = jnp.broadcast_to(gn_ref[:, h : h + 1].astype(f32), (3, HD))
    request = iota((HEADS * 4, HD), 0) % 4
    new_pos = jnp.where(request == 0, len0, jnp.where(request == 1, len1, jnp.where(request == 2, len2, 0)))
    new_cos, new_sin = rope_tables(new_pos.astype(f32))
    scale = HD**-0.5
    new_q = norm_rope(nq[...], q_gain, new_cos, new_sin).astype(bf16)
    new_k = norm_rope(nk[...], k_gain, new_cos, new_sin).astype(bf16)
    self_score = jnp.sum(new_q.astype(f32) * new_k.astype(f32), axis=-1, keepdims=True) * scale
    selfw[...] = jnp.broadcast_to(jnp.exp(self_score), selfw.shape)
    nq[...] = new_q.astype(f32)

    row_req = iota((8, TOK), 0) % 4
    token = t * TOK + iota((8, TOK), 1)
    begin = jnp.where(row_req == 0, 0, jnp.where(row_req == 1, end0, jnp.where(row_req == 2, end1, 0)))
    finish = jnp.where(row_req == 0, end0, jnp.where(row_req == 1, end1, jnp.where(row_req == 2, end2, 0)))
    own_bias = jnp.where((token >= begin) & (token < finish), 0.0, MASKED)
    for k in range(KVH):
        lanes = slice(k * HD, (k + 1) * HD)
        scores = nt_dot(nq[k * 8 : (k + 1) * 8, :].astype(bf16), keys[2, :, lanes]) * scale
        weights = jnp.exp(scores + own_bias)
        x1_out[k, 0:8, :] = jnp.dot(weights.astype(bf16), v_ref[:, lanes], preferred_element_type=f32)
        x1_out[k, 8:16, :] = jnp.broadcast_to(jnp.sum(weights, axis=-1, keepdims=True), (8, HD))
    x1_in[pl.ds(t, 1)] = x1_out[pl.ds(t, 1)]
    c1 = [
        send(x1_out.at[(t + d) % NT], x1_in.at[t], x1_send.at[d - 1], x1_recv.at[d - 1], tp_dev((t + d) % NT))
        for d in range(1, NT)
    ]

    for copy in s1:
        copy.wait_recv()
    block = piece_in[...].reshape(NP * 16, 3 * 128).astype(f32)
    for n in range(3):
        turned = jnp.transpose(block[:, n * 128 : (n + 1) * 128])
        gathered[pl.ds(z, 1), n * CHUNK : (n + 1) * CHUNK, :] = turned[:CHUNK, :].astype(bf16)[None]

    ring = {}

    def ring_step(s):
        if s > 1:
            for copy in ring[s - 1]:
                copy.wait_recv()
        if s > NZ // 2:
            return
        copies = []
        slot = gathered.at[(z + NZ - s + 1) % NZ]
        copies.append(send(slot, slot, right_send.at[s - 1], right_recv.at[s - 1], z_dev(z + 1)))
        if s < NZ // 2:
            slot = gathered.at[(z + s - 1) % NZ]
            copies.append(send(slot, slot, left_send.at[s - 1], left_recv.at[s - 1], z_dev(z + NZ - 1)))
        ring[s] = copies

    ring_step(1)

    low = iota((8, 1024), 0) < 4
    fold[...] = jnp.zeros_like(fold)
    fold[0:3, :] = resid_ref[:, :1024].astype(f32)
    fold[4:7, :] = resid_ref[:, 1024:].astype(f32)
    key_index = (t - 2) * TOK + iota((TOK, 3 * TOK), 1)
    query_index = t * TOK + iota((TOK, 3 * TOK), 0)
    allowed = (key_index >= start_of(query_index)) & (key_index <= query_index)
    bias[...] = jnp.where(allowed, 0.0, MASKED)
    gate_rows = jax.nn.sigmoid(gate_ref[...].astype(f32))
    gates[...] = jnp.transpose(jnp.concatenate([gate_rows, jnp.zeros((120, TOK), f32)], axis=0))

    for copy in c1:
        copy.wait_recv()
    both = x1_in[0] + x1_in[1] + x1_in[2] + x1_in[3]
    mine = pl.ds(pl.multiple_of(t * 8, 8), 8)
    own_self = selfw[mine, :]
    mixed = both[0:8] + own_self * nv[mine, :]
    attended = (mixed / (both[8:16] + own_self) * jax.nn.sigmoid(ngate[mine, :])).astype(bf16)
    first = jnp.dot(attended, wo_ref[0:HD, :], preferred_element_type=f32)
    second = jnp.dot(attended, wo_ref[HD : 2 * HD, :], preferred_element_type=f32)
    sums = first + roll(second, 4, 0)
    x2[pl.ds(t, 1)] = jnp.where(low, sums[:, :1024], roll(sums[:, 1024:], 4, 0))[None]
    c2 = [
        send(x2.at[t], x2.at[t], x2_send.at[d - 1], x2_recv.at[d - 1], tp_dev((t + d) % NT))
        for d in range(1, NT)
    ]
    ring_step(2)

    for d in (1, 2):

        @pl.when(t >= d)
        def _(d=d):
            for n, (src, dst) in enumerate(((keys.at[2], keys.at[2 - d]), (v_ref, vals.at[2 - d]))):
                pltpu.make_async_remote_copy(
                    src_ref=src,
                    dst_ref=dst,
                    send_sem=kv_send.at[d - 1, n],
                    recv_sem=kv_recv.at[d - 1, n],
                    device_id=tp_dev(lax.rem(t + d, NT)),
                    device_id_type=mesh_id,
                ).wait_recv()

    def attend(h):
        lanes = slice(h * HD, (h + 1) * HD)
        kv_lanes = slice(h // 2 * HD, (h // 2 + 1) * HD)
        query = norm_rope(q_ref[:, lanes].astype(f32), q_gain, cos_t[...], sin_t[...]).astype(bf16)
        total = jnp.zeros((TOK, 1), f32)
        mixed = jnp.zeros((TOK, HD), f32)
        for b in range(3):
            scores = nt_dot(query, keys[b, :, kv_lanes]) * scale
            weights = jnp.exp(scores + bias[:, b * TOK : (b + 1) * TOK])
            total = total + jnp.sum(weights, axis=-1, keepdims=True)
            value = v_ref[:, kv_lanes] if b == 2 else vals[b, :, kv_lanes]
            mixed = mixed + jnp.dot(weights.astype(bf16), value, preferred_element_type=f32)
        out_ref[:, lanes] = (mixed / total * gates[:, h : h + 1]).astype(bf16)

    attend(0)
    attend(1)

    for copy in c2:
        copy.wait_recv()
    hidden = fold[...] + (x2[0] + x2[1] + x2[2] + x2[3])
    squares = jnp.sum(hidden * hidden, axis=-1, keepdims=True)
    squares = jnp.broadcast_to(squares, (8, 128))
    mean_sq = ((squares + roll(squares, 4, 0)) / 2048.0)[:, 0:1]
    gain = jnp.where(low, ng_ref[:, :1024], ng_ref[:, 1024:])
    normed = (hidden * lax.rsqrt(mean_sq + norm_eps) * gain).astype(bf16).astype(f32)
    xa[pl.ds(p, 1)] = swap_halves(normed)[None]
    ca = [
        send(xa.at[p], xa.at[p], xa_send.at[d - 1], xa_recv.at[d - 1], plane_dev((p + d) % NP))
        for d in range(1, NP)
    ]
    for s in range(3, NZ // 2 + 2):
        ring_step(s)
        if s <= 5:
            attend(2 * s - 4)
            attend(2 * s - 3)

    for copy in ca:
        copy.wait_recv()
    tokens = xa[...].reshape(NP * 8, 1024).astype(bf16)
    parts = []
    for n in range(2):
        halves = []
        for h in range(2):
            total = jnp.zeros((NP * 8, CHUNK), f32)
            for j in range(NZ // 2):
                total = total + nt_dot(
                    tokens[:, j * 128 : (j + 1) * 128],
                    gathered[2 * j + h, n * CHUNK : (n + 1) * CHUNK, :],
                )
            halves.append(total)
        parts.append(halves)
    shift = NP * 8 - 4
    unit_gate = parts[0][0] + roll(jnp.concatenate([parts[0][1], jnp.zeros((NP * 8, 32), f32)], axis=1), shift, 0)[:, :CHUNK]
    unit_up = parts[1][0] + roll(jnp.concatenate([parts[1][1], jnp.zeros((NP * 8, 32), f32)], axis=1), shift, 0)[:, :CHUNK]
    units = (unit_gate / (1.0 + jnp.exp(-unit_gate)) * unit_up).astype(bf16)
    low_rows = iota((NP * 8, 128), 0) % 8 < 4
    for j in range(NZ // 2):
        even = jnp.dot(units, gathered[2 * j, 2 * CHUNK : 3 * CHUNK, :], preferred_element_type=f32)
        odd = jnp.dot(units, gathered[2 * j + 1, 2 * CHUNK : 3 * CHUNK, :], preferred_element_type=f32)
        xb_out[:, :, j * 128 : (j + 1) * 128] = jnp.where(low_rows, even, roll(odd, 4, 0)).reshape(NP, 8, 128)
    xb_in[pl.ds(p, 1)] = xb_out[pl.ds(p, 1)]
    cb = [
        send(xb_out.at[(p + d) % NP], xb_in.at[p], xb_send.at[d - 1], xb_recv.at[d - 1], plane_dev((p + d) % NP))
        for d in range(1, NP)
    ]
    for copy in cb:
        copy.wait_recv()
    total = xb_in[0]
    for i in range(1, NP):
        total = total + xb_in[i]
    xc[pl.ds(t, 1)] = total[None]
    cc = [
        send(xc.at[t], xc.at[t], xc_send.at[d - 1], xc_recv.at[d - 1], tp_dev((t + d) % NT))
        for d in range(1, NT)
    ]
    for copy in cc:
        copy.wait_recv()
    result = (hidden + swap_halves(xc[0] + xc[1] + xc[2] + xc[3])).astype(bf16)
    dec_ref[:, :1024] = result[0:3]
    dec_ref[:, 1024:] = result[4:7]

    for copy in started:
        copy.wait_send()
    for d in (1, 2):

        @pl.when(t + d < NT)
        def _(d=d):
            for n, (src, dst) in enumerate(((keys.at[2], keys.at[2 - d]), (v_ref, vals.at[2 - d]))):
                pltpu.make_async_remote_copy(
                    src_ref=src,
                    dst_ref=dst,
                    send_sem=kv_send.at[d - 1, n],
                    recv_sem=kv_recv.at[d - 1, n],
                    device_id=tp_dev(lax.rem(t + d, NT)),
                    device_id_type=mesh_id,
                ).wait_send()


def local(
    q_pre,
    gate_pre,
    k_pre,
    v_pre,
    q_gain,
    k_gain,
    lengths,
    q_new,
    gate_new,
    k_new,
    v_new,
    resid,
    w_out,
    norm_gain,
    w_gate,
    w_up,
    w_down,
):
    vmem = pl.BlockSpec(memory_space=pltpu.VMEM)
    dma = pltpu.SemaphoreType.DMA
    return pl.pallas_call(
        kernel,
        out_shape=(
            jax.ShapeDtypeStruct((TOK, HEADS * HD), bf16),
            jax.ShapeDtypeStruct((3, 2048), bf16),
        ),
        in_specs=[pl.BlockSpec(memory_space=pltpu.SMEM)] + [vmem] * 16,
        out_specs=(vmem, vmem),
        scratch_shapes=[
            pltpu.VMEM((3, TOK, KVH * HD), bf16),
            pltpu.VMEM((2, TOK, KVH * HD), bf16),
            pltpu.VMEM((TOK, 3 * TOK), f32),
            pltpu.VMEM((HEADS * 4, HD), f32),
            pltpu.VMEM((HEADS * 4, HD), f32),
            pltpu.VMEM((HEADS * 4, HD), f32),
            pltpu.VMEM((HEADS * 4, HD), f32),
            pltpu.VMEM((HEADS * 4, HD), f32),
            pltpu.VMEM((8, 1024), f32),
            pltpu.VMEM((NP, 16, 384), bf16),
            pltpu.VMEM((NP, 16, 384), bf16),
            pltpu.VMEM((NZ, 3 * CHUNK, 128), bf16),
            pltpu.VMEM((NT, 16, 128), f32),
            pltpu.VMEM((NT, 16, 128), f32),
            pltpu.VMEM((NT, 8, 1024), f32),
            pltpu.VMEM((NP, 8, 1024), f32),
            pltpu.VMEM((NP, 8, 1024), f32),
            pltpu.VMEM((NP, 8, 1024), f32),
            pltpu.VMEM((NT, 8, 1024), f32),
            pltpu.VMEM((TOK, HD), f32),
            pltpu.VMEM((TOK, HD), f32),
            pltpu.VMEM((TOK, 128), f32),
            dma((NP - 1,)),
            dma((NP - 1,)),
            dma((2, 2)),
            dma((2, 2)),
            dma((NT - 1,)),
            dma((NT - 1,)),
            dma((NT - 1,)),
            dma((NT - 1,)),
            dma((NP - 1,)),
            dma((NP - 1,)),
            dma((NP - 1,)),
            dma((NP - 1,)),
            dma((NT - 1,)),
            dma((NT - 1,)),
            dma((NZ // 2,)),
            dma((NZ // 2,)),
            dma((NZ // 2 - 1,)),
            dma((NZ // 2 - 1,)),
        ],
        compiler_params=pltpu.CompilerParams(
            collective_id=0, has_side_effects=True, vmem_limit_bytes=40 * 1024 * 1024
        ),
    )(
        lengths,
        q_pre,
        gate_pre.T,
        k_pre,
        v_pre,
        q_gain.reshape(1, HD),
        k_gain.reshape(1, HD),
        q_new,
        gate_new,
        k_new,
        v_new,
        resid,
        w_out,
        norm_gain.reshape(1, 2048),
        w_gate,
        w_up,
        w_down.T,
    )


def solution(mesh):
    wide = jax.sharding.Mesh(
        mesh.devices.reshape(NX, NZ, NY, 2, 2), ("xlo", "z", "y", "xhi", "core")
    )
    return jax.shard_map(
        local,
        mesh=wide,
        in_specs=(
            P(req + tp, None),
            P(req + tp, None),
            P(req + tp, None),
            P(req + tp, None),
            P(),
            P(),
            P(req, None),
            P(req, None),
            P(req, None),
            P(req, None),
            P(req, None),
            P(req, None),
            P(tp, None),
            P(),
            P(req, tp),
            P(req, tp),
            P(tp, req),
        ),
        out_specs=(P(req + tp, None), P(req, None)),
        check_vma=False,
    )
```

time: 242 us -> 82.1 us (0.34)
  the two profiles are of different devices: /device:TPU:4 before, /device:TPU:1 now
where the time goes in v2:
time: 82.1 us; the launch traced here: 81.4 us
  Pallas kernels  67.1 us (82%)
  local copies, waits for them, and re-layouts  13.6 us (17%)
    pallas_call x1, Pallas kernels, local(): pl.pallas_call(kernel, out_shape=(jax.ShapeDtypeStruct((TOK, HEADS * HD),...  67.1 us
    unnamed x36, local copies, waits for them, and re-layouts  13.6 us

profile of v2, /device:TPU:1, one launch (start us, length us, event | category | flops | bytes accessed | tf_op | source)
XLA Modules:
  0.0 81.4 jit_solution(5073770243856060212)
XLA Ops:
  0.6 0.0 copy-start.8
  0.6 0.0 copy-start.13
  0.7 0.7 copy-done.8
  1.3 0.0 copy-done.13
  1.3 0.0 copy-start
  1.3 1.2 %copy-done = bf16[256,2048]{1,0:T(8,128)(2,1)S(1)} copy-done((bf16[256,2048]{1,0:T(8,128)(2,1)S(1)}, bf16[256,2048]{1,0:T(8,128)(2,1)}, u32[]{:S(2)}) %copy-start) | copy-done | bytes 1048600
  2.6 0.0 copy-start.1
  2.6 0.9 %copy-done.1 = bf16[128,1024]{1,0:T(8,128)(2,1)S(1)} copy-done((bf16[128,1024]{1,0:T(8,128)(2,1)S(1)}, bf16[128,1024]{1,0:T(8,128)(2,1)}, u32[]{:S(2)}) %copy-start.1) | copy-done | bytes 262168
  3.5 0.0 copy-start.2
  3.5 0.9 %copy-done.2 = bf16[128,512]{1,0:T(8,128)(2,1)S(1)} copy-done((bf16[128,512]{1,0:T(8,128)(2,1)S(1)}, bf16[128,512]{1,0:T(8,128)(2,1)}, u32[]{:S(2)}) %copy-start.2) | copy-done | bytes 131096
  4.4 0.0 copy-start.3
  4.4 0.9 %copy-done.3 = bf16[128,512]{1,0:T(8,128)(2,1)S(1)} copy-done((bf16[128,512]{1,0:T(8,128)(2,1)S(1)}, bf16[128,512]{1,0:T(8,128)(2,1)}, u32[]{:S(2)}) %copy-start.3) | copy-done | bytes 131096
  5.3 0.0 copy-start.4
  5.3 0.7 copy-done.4
  6.1 0.0 copy-start.5
  6.1 0.7 copy-done.5
  6.8 0.0 copy-start.6
  6.8 0.7 copy-done.6
  7.5 0.0 copy-start.7
  7.5 0.7 copy-done.7
  8.3 0.0 copy-start.9
  8.3 0.7 copy-done.9
  9.0 0.0 copy-start.10
  9.0 0.7 copy-done.10
  9.6 0.0 copy-start.11
  9.6 0.7 copy-done.11
  10.3 0.0 copy-start.12
  10.3 0.7 copy-done.12
  11.0 0.0 copy-start.14
  11.0 0.7 copy-done.14
  11.7 0.0 copy-start.15
  11.7 0.7 copy-done.15
  12.3 0.0 copy-start.16
  12.3 0.7 copy-done.16
  13.0 67.1 %shard_map.176 = (bf16[128,1024]{1,0:T(8,128)(2,1)S(1)}, bf16[3,2048]{1,0:T(4,128)(2,1)S(1)}) custom-call(s32[1,3]{1,0:T(1,128)S(1)} %copy-done.14, bf16[128,1024]{1,0:T(8,128)(2,1)S(1)} %copy-done.1, bf16[8,128]{1,0:T(8,128)(2,1)S(1)} %bitcast.7, bf16[128,512]{1,0:T(8,128)(2,1)S(1)} %copy-done.2, bf16[128,512]{1,0:T(8,128)(2,1)S(1)} %copy-done.3, ...), custom_call_target="tpu_custom_call" | custom-call | tf_op jit(solution)/shard_map/pallas_call | solution.py:433
  80.1 0.7 copy.21
  80.8 0.6 copy.22
Async XLA Ops:
  0.6 0.7 copy-start.8
  0.6 0.7 copy-start.13
  1.3 1.2 %copy-start = (bf16[256,2048]{1,0:T(8,128)(2,1)S(1)}, bf16[256,2048]{1,0:T(8,128)(2,1)}, u32[]{:S(2)}) copy-start(bf16[256,2048]{1,0:T(8,128)(2,1)} %wo_ref.1) | copy-start | bytes 3145732
  2.6 0.9 %copy-start.1 = (bf16[128,1024]{1,0:T(8,128)(2,1)S(1)}, bf16[128,1024]{1,0:T(8,128)(2,1)}, u32[]{:S(2)}) copy-start(bf16[128,1024]{1,0:T(8,128)(2,1)} %q_ref.1) | copy-start | bytes 786436
  3.5 0.9 %copy-start.2 = (bf16[128,512]{1,0:T(8,128)(2,1)S(1)}, bf16[128,512]{1,0:T(8,128)(2,1)}, u32[]{:S(2)}) copy-start(bf16[128,512]{1,0:T(8,128)(2,1)} %k_ref.1) | copy-start | bytes 393220
  4.4 0.9 %copy-start.3 = (bf16[128,512]{1,0:T(8,128)(2,1)S(1)}, bf16[128,512]{1,0:T(8,128)(2,1)}, u32[]{:S(2)}) copy-start(bf16[128,512]{1,0:T(8,128)(2,1)} %v_ref.1) | copy-start | bytes 393220
  5.3 0.7 copy-start.4
  6.1 0.7 copy-start.5
  6.8 0.7 copy-start.6
  7.5 0.7 copy-start.7
  8.3 0.7 copy-start.9
  9.0 0.7 copy-start.10
  9.6 0.7 copy-start.11
  10.3 0.7 copy-start.12
  11.0 0.7 copy-start.14
  11.7 0.7 copy-start.15
  12.3 0.7 copy-start.16

commit v3 on v2

--- a/solution.py
+++ b/solution.py
@@ -18,6 +18,8 @@
 KVH = 4
 TOK = 128
 CHUNK = 96
+CHUNKS = 2
+ROWS = 3 * CHUNK // CHUNKS
 MASKED = -1e30
 f32 = jnp.float32
 bf16 = jnp.bfloat16
@@ -61,24 +63,24 @@
 
 def kernel(
     lengths_ref,
-    q_ref,
-    gate_ref,
-    k_ref,
-    v_ref,
-    qg_ref,
-    kg_ref,
-    qn_ref,
-    gn_ref,
-    kn_ref,
-    vn_ref,
-    resid_ref,
-    wo_ref,
-    ng_ref,
-    wg_ref,
-    wu_ref,
-    wd_ref,
-    out_ref,
-    dec_ref,
+    q_hbm,
+    gate_hbm,
+    k_hbm,
+    v_hbm,
+    qg_hbm,
+    kg_hbm,
+    qn_hbm,
+    gn_hbm,
+    kn_hbm,
+    vn_hbm,
+    resid_hbm,
+    wo_hbm,
+    ng_hbm,
+    wg_hbm,
+    wu_hbm,
+    wd_hbm,
+    out_hbm,
+    dec_hbm,
     keys,
     vals,
     bias,
@@ -101,6 +103,25 @@
     cos_t,
     sin_t,
     gates,
+    q_ref,
+    gate_ref,
+    k_ref,
+    v_ref,
+    qg_ref,
+    kg_ref,
+    qn_ref,
+    gn_ref,
+    kn_ref,
+    vn_ref,
+    resid_ref,
+    wo_ref,
+    ng_ref,
+    wg_ref,
+    wu_ref,
+    wd_ref,
+    out_ref,
+    dec_ref,
+    in_sem,
     s1_send,
     s1_recv,
     kv_send,
@@ -115,10 +136,9 @@
     xb_recv,
     xc_send,
     xc_recv,
-    right_send,
-    right_recv,
-    left_send,
-    left_recv,
+    ring_send,
+    ring_recv,
+    out_sem,
 ):
     xlo, z, y = lax.axis_index("xlo"), lax.axis_index("z"), lax.axis_index("y")
     t = lax.axis_index("xhi") * 2 + lax.axis_index("core")
@@ -132,6 +152,34 @@
 
     def z_dev(i):
         return {"z": i % NZ}
+
+    loads = {}
+    for n, (name, src, dst) in enumerate(
+        (
+            ("wg", wg_hbm, wg_ref),
+            ("wu", wu_hbm, wu_ref),
+            ("wd", wd_hbm, wd_ref),
+            ("k", k_hbm, k_ref),
+            ("qg", qg_hbm, qg_ref),
+            ("kg", kg_hbm, kg_ref),
+            ("v", v_hbm, v_ref),
+            ("qn", qn_hbm, qn_ref),
+            ("kn", kn_hbm, kn_ref),
+            ("vn", vn_hbm, vn_ref),
+            ("gn", gn_hbm, gn_ref),
+            ("resid", resid_hbm, resid_ref),
+            ("gate", gate_hbm, gate_ref),
+            ("wo", wo_hbm, wo_ref),
+            ("ng", ng_hbm, ng_ref),
+            ("q", q_hbm, q_ref),
+        )
+    ):
+        loads[name] = pltpu.make_async_copy(src, dst, in_sem.at[n])
+        loads[name].start()
+
+    def arrive(*wanted):
+        for name in wanted:
+            loads[name].wait()
 
     barrier = pltpu.get_barrier_semaphore()
     mesh_id = pl.DeviceIdType.MESH
@@ -139,8 +187,8 @@
         pl.semaphore_signal(barrier, inc=1, device_id=tp_dev((t + d) % NT), device_id_type=mesh_id)
     for d in range(1, NP):
         pl.semaphore_signal(barrier, inc=1, device_id=plane_dev((p + d) % NP), device_id_type=mesh_id)
-    pl.semaphore_signal(barrier, inc=1, device_id=z_dev(z + 1), device_id_type=mesh_id)
-    pl.semaphore_signal(barrier, inc=1, device_id=z_dev(z + NZ - 1), device_id_type=mesh_id)
+    for d in (1, 2, NZ - 2, NZ - 1):
+        pl.semaphore_signal(barrier, inc=1, device_id=z_dev(z + d), device_id_type=mesh_id)
 
     started = []
 
@@ -157,6 +205,7 @@
         started.append(copy)
         return copy
 
+    arrive("wg", "wu", "wd")
     for n, ref in enumerate((wg_ref, wu_ref, wd_ref)):
         whole = ref[...].astype(f32)
         width = whole.shape[1]
@@ -165,7 +214,7 @@
             piece_out[i, :, n * 128 : (n + 1) * 128] = part[:, :128].astype(bf16)
     piece_in[pl.ds(p, 1)] = piece_out[pl.ds(p, 1)]
 
-    pl.semaphore_wait(barrier, NT - 1 + NP - 1 + 2)
+    pl.semaphore_wait(barrier, NT - 1 + NP - 1 + 4)
     s1 = [
         send(piece_out.at[(p + d) % NP], piece_in.at[p], s1_send.at[d - 1], s1_recv.at[d - 1], plane_dev((p + d) % NP))
         for d in range(1, NP)
@@ -183,6 +232,7 @@
     cos_t[...] = cosine
     sin_t[...] = sine
 
+    arrive("k", "qg", "kg", "v")
     k_gain = kg_ref[...]
     q_gain = qg_ref[...]
     for k in range(KVH):
@@ -207,6 +257,7 @@
             keys[2 - d] = jnp.zeros((TOK, KVH * HD), bf16)
             vals[2 - d] = jnp.zeros((TOK, KVH * HD), bf16)
 
+    arrive("qn", "kn", "vn", "gn")
     for ref in (nq, nk, nv, ngate):
         ref[...] = jnp.zeros_like(ref)
     for h in range(HEADS):
@@ -251,24 +302,34 @@
         turned = jnp.transpose(block[:, n * 128 : (n + 1) * 128])
         gathered[pl.ds(z, 1), n * CHUNK : (n + 1) * CHUNK, :] = turned[:CHUNK, :].astype(bf16)[None]
 
-    ring = {}
-
-    def ring_step(s):
-        if s > 1:
-            for copy in ring[s - 1]:
-                copy.wait_recv()
-        if s > NZ // 2:
-            return
-        copies = []
-        slot = gathered.at[(z + NZ - s + 1) % NZ]
-        copies.append(send(slot, slot, right_send.at[s - 1], right_recv.at[s - 1], z_dev(z + 1)))
-        if s < NZ // 2:
-            slot = gathered.at[(z + s - 1) % NZ]
-            copies.append(send(slot, slot, left_send.at[s - 1], left_recv.at[s - 1], z_dev(z + NZ - 1)))
-        ring[s] = copies
+    far = {}
+    near = []
+
+    def pass_on(step, chunk, backward):
+        key = (step, chunk, backward)
+        if step > 1:
+            far[(step - 1, chunk, backward)].wait_recv()
+        sign = NZ - 1 if backward else 1
+        origin = (z + (NZ - sign) * 2 * (step - 1)) % NZ
+        slot = gathered.at[origin, pl.ds(chunk * ROWS, ROWS)]
+        for reach in (2, 1):
+            if backward and step == 4 and reach == 2:
+                continue
+            n = (((step - 1) * CHUNKS + chunk) * 2 + int(backward)) * 2 + reach - 1
+            copy = send(slot, slot, ring_send.at[n], ring_recv.at[n], z_dev(z + sign * reach))
+            if reach == 2 and step < 4:
+                far[key] = copy
+            else:
+                near.append(copy)
+
+    def ring_step(step):
+        for chunk in range(CHUNKS):
+            for backward in (False, True):
+                pass_on(step, chunk, backward)
 
     ring_step(1)
 
+    arrive("resid", "gate")
     low = iota((8, 1024), 0) < 4
     fold[...] = jnp.zeros_like(fold)
     fold[0:3, :] = resid_ref[:, :1024].astype(f32)
@@ -280,6 +341,7 @@
     gate_rows = jax.nn.sigmoid(gate_ref[...].astype(f32))
     gates[...] = jnp.transpose(jnp.concatenate([gate_rows, jnp.zeros((120, TOK), f32)], axis=0))
 
+    arrive("wo")
     for copy in c1:
         copy.wait_recv()
     both = x1_in[0] + x1_in[1] + x1_in[2] + x1_in[3]
@@ -290,13 +352,11 @@
     first = jnp.dot(attended, wo_ref[0:HD, :], preferred_element_type=f32)
     second = jnp.dot(attended, wo_ref[HD : 2 * HD, :], preferred_element_type=f32)
     sums = first + roll(second, 4, 0)
-    x2[pl.ds(t, 1)] = jnp.where(low, sums[:, :1024], roll(sums[:, 1024:], 4, 0))[None]
+    x2[pl.ds(t, 1)] = jnp.where(low, sums[:, :1024], roll(sums[:, 1024:], 4, 0)).astype(bf16)[None]
     c2 = [
         send(x2.at[t], x2.at[t], x2_send.at[d - 1], x2_recv.at[d - 1], tp_dev((t + d) % NT))
         for d in range(1, NT)
     ]
-    ring_step(2)
-
     for d in (1, 2):
 
         @pl.when(t >= d)
@@ -311,6 +371,7 @@
                     device_id_type=mesh_id,
                 ).wait_recv()
 
+    arrive("q", "ng")
     def attend(h):
         lanes = slice(h * HD, (h + 1) * HD)
         kv_lanes = slice(h // 2 * HD, (h // 2 + 1) * HD)
@@ -326,30 +387,38 @@
         out_ref[:, lanes] = (mixed / total * gates[:, h : h + 1]).astype(bf16)
 
     attend(0)
+    ring_step(2)
     attend(1)
 
     for copy in c2:
         copy.wait_recv()
-    hidden = fold[...] + (x2[0] + x2[1] + x2[2] + x2[3])
+    attn = x2[0].astype(f32) + x2[1].astype(f32) + x2[2].astype(f32) + x2[3].astype(f32)
+    hidden = fold[...] + attn
     squares = jnp.sum(hidden * hidden, axis=-1, keepdims=True)
     squares = jnp.broadcast_to(squares, (8, 128))
     mean_sq = ((squares + roll(squares, 4, 0)) / 2048.0)[:, 0:1]
     gain = jnp.where(low, ng_ref[:, :1024], ng_ref[:, 1024:])
-    normed = (hidden * lax.rsqrt(mean_sq + norm_eps) * gain).astype(bf16).astype(f32)
-    xa[pl.ds(p, 1)] = swap_halves(normed)[None]
+    normed = hidden * lax.rsqrt(mean_sq + norm_eps) * gain
+    xa[pl.ds(p, 1)] = swap_halves(normed).astype(bf16)[None]
     ca = [
         send(xa.at[p], xa.at[p], xa_send.at[d - 1], xa_recv.at[d - 1], plane_dev((p + d) % NP))
         for d in range(1, NP)
     ]
-    for s in range(3, NZ // 2 + 2):
-        ring_step(s)
-        if s <= 5:
-            attend(2 * s - 4)
-            attend(2 * s - 3)
+    attend(2)
+    ring_step(3)
+    attend(3)
+    attend(4)
+    ring_step(4)
+    for h in range(5, HEADS):
+        attend(h)
+    result_copy = pltpu.make_async_copy(out_ref, out_hbm, out_sem.at[0])
+    result_copy.start()
+    for copy in near:
+        copy.wait_recv()
 
     for copy in ca:
         copy.wait_recv()
-    tokens = xa[...].reshape(NP * 8, 1024).astype(bf16)
+    tokens = xa[...].astype(f32).reshape(NP * 8, 1024).astype(bf16)
     parts = []
     for n in range(2):
         halves = []
@@ -370,7 +439,7 @@
     for j in range(NZ // 2):
         even = jnp.dot(units, gathered[2 * j, 2 * CHUNK : 3 * CHUNK, :], preferred_element_type=f32)
         odd = jnp.dot(units, gathered[2 * j + 1, 2 * CHUNK : 3 * CHUNK, :], preferred_element_type=f32)
-        xb_out[:, :, j * 128 : (j + 1) * 128] = jnp.where(low_rows, even, roll(odd, 4, 0)).reshape(NP, 8, 128)
+        xb_out[:, :, j * 128 : (j + 1) * 128] = jnp.where(low_rows, even, roll(odd, 4, 0)).reshape(NP, 8, 128).astype(bf16)
     xb_in[pl.ds(p, 1)] = xb_out[pl.ds(p, 1)]
     cb = [
         send(xb_out.at[(p + d) % NP], xb_in.at[p], xb_send.at[d - 1], xb_recv.at[d - 1], plane_dev((p + d) % NP))
@@ -378,22 +447,27 @@
     ]
     for copy in cb:
         copy.wait_recv()
-    total = xb_in[0]
+    total = xb_in[0].astype(f32)
     for i in range(1, NP):
-        total = total + xb_in[i]
-    xc[pl.ds(t, 1)] = total[None]
+        total = total + xb_in[i].astype(f32)
+    xc[pl.ds(t, 1)] = total.astype(bf16)[None]
     cc = [
         send(xc.at[t], xc.at[t], xc_send.at[d - 1], xc_recv.at[d - 1], tp_dev((t + d) % NT))
         for d in range(1, NT)
     ]
     for copy in cc:
         copy.wait_recv()
-    result = (hidden + swap_halves(xc[0] + xc[1] + xc[2] + xc[3])).astype(bf16)
+    down = xc[0].astype(f32) + xc[1].astype(f32) + xc[2].astype(f32) + xc[3].astype(f32)
+    result = (hidden + swap_halves(down)).astype(bf16)
     dec_ref[:, :1024] = result[0:3]
     dec_ref[:, 1024:] = result[4:7]
+    last_copy = pltpu.make_async_copy(dec_ref, dec_hbm, out_sem.at[1])
+    last_copy.start()
 
     for copy in started:
         copy.wait_send()
+    result_copy.wait()
+    last_copy.wait()
     for d in (1, 2):
 
         @pl.when(t + d < NT)
@@ -428,7 +502,6 @@
     w_up,
     w_down,
 ):
-    vmem = pl.BlockSpec(memory_space=pltpu.VMEM)
     dma = pltpu.SemaphoreType.DMA
     return pl.pallas_call(
         kernel,
@@ -436,8 +509,8 @@
             jax.ShapeDtypeStruct((TOK, HEADS * HD), bf16),
             jax.ShapeDtypeStruct((3, 2048), bf16),
         ),
-        in_specs=[pl.BlockSpec(memory_space=pltpu.SMEM)] + [vmem] * 16,
-        out_specs=(vmem, vmem),
+        in_specs=[pl.BlockSpec(memory_space=pltpu.SMEM)] + [pl.BlockSpec(memory_space=pltpu.HBM)] * 16,
+        out_specs=(pl.BlockSpec(memory_space=pltpu.HBM),) * 2,
         scratch_shapes=[
             pltpu.VMEM((3, TOK, KVH * HD), bf16),
             pltpu.VMEM((2, TOK, KVH * HD), bf16),
@@ -453,14 +526,33 @@
             pltpu.VMEM((NZ, 3 * CHUNK, 128), bf16),
             pltpu.VMEM((NT, 16, 128), f32),
             pltpu.VMEM((NT, 16, 128), f32),
-            pltpu.VMEM((NT, 8, 1024), f32),
-            pltpu.VMEM((NP, 8, 1024), f32),
-            pltpu.VMEM((NP, 8, 1024), f32),
-            pltpu.VMEM((NP, 8, 1024), f32),
-            pltpu.VMEM((NT, 8, 1024), f32),
+            pltpu.VMEM((NT, 8, 1024), bf16),
+            pltpu.VMEM((NP, 8, 1024), bf16),
+            pltpu.VMEM((NP, 8, 1024), bf16),
+            pltpu.VMEM((NP, 8, 1024), bf16),
+            pltpu.VMEM((NT, 8, 1024), bf16),
             pltpu.VMEM((TOK, HD), f32),
             pltpu.VMEM((TOK, HD), f32),
             pltpu.VMEM((TOK, 128), f32),
+            pltpu.VMEM((TOK, HEADS * HD), bf16),
+            pltpu.VMEM((HEADS, TOK), bf16),
+            pltpu.VMEM((TOK, KVH * HD), bf16),
+            pltpu.VMEM((TOK, KVH * HD), bf16),
+            pltpu.VMEM((1, HD), f32),
+            pltpu.VMEM((1, HD), f32),
+            pltpu.VMEM((3, HEADS * HD), bf16),
+            pltpu.VMEM((3, HEADS), bf16),
+            pltpu.VMEM((3, KVH * HD), bf16),
+            pltpu.VMEM((3, KVH * HD), bf16),
+            pltpu.VMEM((3, 2048), bf16),
+            pltpu.VMEM((2 * HD, 2048), bf16),
+            pltpu.VMEM((1, 2048), f32),
+            pltpu.VMEM((16, 768), bf16),
+            pltpu.VMEM((16, 768), bf16),
+            pltpu.VMEM((16, 768), bf16),
+            pltpu.VMEM((TOK, HEADS * HD), bf16),
+            pltpu.VMEM((3, 2048), bf16),
+            dma((16,)),
             dma((NP - 1,)),
             dma((NP - 1,)),
             dma((2, 2)),
@@ -475,13 +567,12 @@
             dma((NP - 1,)),
             dma((NT - 1,)),
             dma((NT - 1,)),
-            dma((NZ // 2,)),
-            dma((NZ // 2,)),
-            dma((NZ // 2 - 1,)),
-            dma((NZ // 2 - 1,)),
+            dma((4 * CHUNKS * 4,)),
+            dma((4 * CHUNKS * 4,)),
+            dma((2,)),
         ],
         compiler_params=pltpu.CompilerParams(
-            collective_id=0, has_side_effects=True, vmem_limit_bytes=40 * 1024 * 1024
+            collective_id=0, has_side_effects=True, vmem_limit_bytes=60 * 1024 * 1024
         ),
     )(
         lengths,

time: 82.1 us -> 58.9 us (0.72)
  local copies, waits for them, and re-layouts: 13.6 us -> 2.28 us
  Pallas kernels: 67.1 us -> 55.8 us
    unnamed x36 -> x4, local copies, waits for them, and re-layouts: 13.6 us -> 2.28 us
    pallas_call x1, Pallas kernels: 67.1 us -> 55.8 us  [local(): pl.pallas_call(kernel, out_shape=(jax.ShapeDtypeStruct((TOK, HEADS * HD),...]
where the time goes in v3:
time: 58.9 us; the launch traced here: 58.8 us
  Pallas kernels  55.8 us (95%)
  local copies, waits for them, and re-layouts  2.28 us (4%)
  between operations  0.65 us (1%)
    pallas_call x1, Pallas kernels, local(): pl.pallas_call(kernel, out_shape=(jax.ShapeDtypeStruct((TOK, HEADS * HD),...  55.8 us
    unnamed x4, local copies, waits for them, and re-layouts  2.28 us

profile of v3, /device:TPU:1, one launch (start us, length us, event | category | flops | bytes accessed | tf_op | source)
XLA Modules:
  0.0 58.8 jit_solution(3262603701380765103)
XLA Ops:
  0.6 55.8 %shard_map.176 = (bf16[128,1024]{1,0:T(8,128)(2,1)}, bf16[3,2048]{1,0:T(4,128)(2,1)}) custom-call(s32[1,3]{1,0:T(1,128)} %lengths_ref.1, bf16[128,1024]{1,0:T(8,128)(2,1)} %q_hbm.1, bf16[8,128]{1,0:T(8,128)(2,1)} %bitcast.7, bf16[128,512]{1,0:T(8,128)(2,1)} %k_hbm.1, bf16[128,512]{1,0:T(8,128)(2,1)} %v_hbm.1, f32[1,128]{1,0:T(1,128)} %bitcast.8, ...), custom_call_target="tpu_custom_call" | custom-call | tf_op jit(solution)/shard_map/pallas_call | solution.py:506
  56.5 0.0 copy-start
  56.5 1.7 %copy.21 = bf16[128,1024]{1,0:T(8,128)(2,1)} copy(bf16[128,1024]{1,0:T(8,128)(2,1)} %get-tuple-element.4) | data formatting | bytes 524288
  58.2 0.0 copy-done
  58.2 0.6 %copy.22 = bf16[3,2048]{1,0:T(4,128)(2,1)} copy(bf16[3,2048]{1,0:T(4,128)(2,1)S(1)} %copy-done) | data formatting | bytes 24576
Async XLA Ops:
  56.5 1.7 %copy-start = (bf16[3,2048]{1,0:T(4,128)(2,1)S(1)}, bf16[3,2048]{1,0:T(4,128)(2,1)}, u32[]{:S(2)}) copy-start(bf16[3,2048]{1,0:T(4,128)(2,1)} %get-tuple-element.5) | copy-start | bytes 36868

commit v4 on v3

--- a/solution.py
+++ b/solution.py
@@ -37,13 +37,12 @@
     return lax.dot_general(a, b, (((1,), (1,)), ((), ())), preferred_element_type=f32)
 
 
-def rope_tables(position):
+def angle_tables(position):
     lane = iota(position.shape, 1)
     index = (lane % 64).astype(f32)
     freqs = jnp.exp(index * (-2.0 / HD * 13.815510557964274))
     angles = position * freqs
-    sine = jnp.sin(angles)
-    return jnp.cos(angles), jnp.where(lane < 64, -sine, sine)
+    return jnp.cos(angles), jnp.sin(angles)
 
 
 def norm_rope(values, gain, cosine, sine):
@@ -214,12 +213,6 @@
             piece_out[i, :, n * 128 : (n + 1) * 128] = part[:, :128].astype(bf16)
     piece_in[pl.ds(p, 1)] = piece_out[pl.ds(p, 1)]
 
-    pl.semaphore_wait(barrier, NT - 1 + NP - 1 + 4)
-    s1 = [
-        send(piece_out.at[(p + d) % NP], piece_in.at[p], s1_send.at[d - 1], s1_recv.at[d - 1], plane_dev((p + d) % NP))
-        for d in range(1, NP)
-    ]
-
     len0, len1, len2 = lengths_ref[0, 0], lengths_ref[0, 1], lengths_ref[0, 2]
     end0, end1 = len0, len0 + len1
     end2 = end1 + len2
@@ -227,10 +220,13 @@
     def start_of(index):
         return jnp.where(index >= end1, end1, jnp.where(index >= end0, end0, 0))
 
-    own_index = t * TOK + iota((TOK, 128), 0)
-    cosine, sine = rope_tables((own_index - start_of(own_index)).astype(f32))
-    cos_t[...] = cosine
-    sin_t[...] = sine
+    left = iota((TOK // 2, 128), 1) < 64
+    own_index = t * TOK + iota((TOK // 2, 128), 0) + jnp.where(left, 0, TOK // 2)
+    for ref, packed, sign in zip((cos_t, sin_t), angle_tables((own_index - start_of(own_index)).astype(f32)), (1.0, -1.0)):
+        turned = roll(packed, 64, 1)
+        ref[: TOK // 2, :] = jnp.where(left, sign * packed, turned)
+        ref[TOK // 2 :, :] = jnp.where(left, sign * turned, packed)
+    cosine, sine = cos_t[...], sin_t[...]
 
     arrive("k", "qg", "kg", "v")
     k_gain = kg_ref[...]
@@ -238,25 +234,6 @@
     for k in range(KVH):
         lanes = slice(k * HD, (k + 1) * HD)
         keys[2, :, lanes] = norm_rope(k_ref[:, lanes].astype(f32), k_gain, cosine, sine).astype(bf16)
-    for d in (1, 2):
-
-        @pl.when(t + d < NT)
-        def _(d=d):
-            for n, (src, dst) in enumerate(((keys.at[2], keys.at[2 - d]), (v_ref, vals.at[2 - d]))):
-                pltpu.make_async_remote_copy(
-                    src_ref=src,
-                    dst_ref=dst,
-                    send_sem=kv_send.at[d - 1, n],
-                    recv_sem=kv_recv.at[d - 1, n],
-                    device_id=tp_dev(lax.rem(t + d, NT)),
-                    device_id_type=mesh_id,
-                ).start()
-
-        @pl.when(t < d)
-        def _(d=d):
-            keys[2 - d] = jnp.zeros((TOK, KVH * HD), bf16)
-            vals[2 - d] = jnp.zeros((TOK, KVH * HD), bf16)
-
     arrive("qn", "kn", "vn", "gn")
     for ref in (nq, nk, nv, ngate):
         ref[...] = jnp.zeros_like(ref)
@@ -268,9 +245,12 @@
         nk[rows, :] = kn_ref[:, kv_lanes].astype(f32)
         nv[rows, :] = vn_ref[:, kv_lanes].astype(f32)
         ngate[rows, :] = jnp.broadcast_to(gn_ref[:, h : h + 1].astype(f32), (3, HD))
-    request = iota((HEADS * 4, HD), 0) % 4
+    request = iota((8, HD), 0) % 4
     new_pos = jnp.where(request == 0, len0, jnp.where(request == 1, len1, jnp.where(request == 2, len2, 0)))
-    new_cos, new_sin = rope_tables(new_pos.astype(f32))
+    new_cos, new_sin = angle_tables(new_pos.astype(f32))
+    new_sin = jnp.where(iota((8, HD), 1) < 64, -new_sin, new_sin)
+    new_cos = jnp.concatenate([new_cos] * 4, axis=0)
+    new_sin = jnp.concatenate([new_sin] * 4, axis=0)
     scale = HD**-0.5
     new_q = norm_rope(nq[...], q_gain, new_cos, new_sin).astype(bf16)
     new_k = norm_rope(nk[...], k_gain, new_cos, new_sin).astype(bf16)
@@ -290,10 +270,35 @@
         x1_out[k, 0:8, :] = jnp.dot(weights.astype(bf16), v_ref[:, lanes], preferred_element_type=f32)
         x1_out[k, 8:16, :] = jnp.broadcast_to(jnp.sum(weights, axis=-1, keepdims=True), (8, HD))
     x1_in[pl.ds(t, 1)] = x1_out[pl.ds(t, 1)]
+    pl.semaphore_wait(barrier, NT - 1 + NP - 1 + 4)
+    s1 = [
+        send(piece_out.at[(p + d) % NP], piece_in.at[p], s1_send.at[d - 1], s1_recv.at[d - 1], plane_dev((p + d) % NP))
+        for d in range(1, NP)
+    ]
+
     c1 = [
         send(x1_out.at[(t + d) % NT], x1_in.at[t], x1_send.at[d - 1], x1_recv.at[d - 1], tp_dev((t + d) % NT))
         for d in range(1, NT)
     ]
+    for d in (1, 2):
+
+        @pl.when(t + d < NT)
+        def _(d=d):
+            for n, (src, dst) in enumerate(((keys.at[2], keys.at[2 - d]), (v_ref, vals.at[2 - d]))):
+                pltpu.make_async_remote_copy(
+                    src_ref=src,
+                    dst_ref=dst,
+                    send_sem=kv_send.at[d - 1, n],
+                    recv_sem=kv_recv.at[d - 1, n],
+                    device_id=tp_dev(lax.rem(t + d, NT)),
+                    device_id_type=mesh_id,
+                ).start()
+
+        @pl.when(t < d)
+        def _(d=d):
+            keys[2 - d] = jnp.zeros((TOK, KVH * HD), bf16)
+            vals[2 - d] = jnp.zeros((TOK, KVH * HD), bf16)
+
 
     for copy in s1:
         copy.wait_recv()
@@ -320,7 +325,7 @@
             if reach == 2 and step < 4:
                 far[key] = copy
             else:
-                near.append(copy)
+                near.append((step, copy))
 
     def ring_step(step):
         for chunk in range(CHUNKS):
@@ -386,8 +391,8 @@
             mixed = mixed + jnp.dot(weights.astype(bf16), value, preferred_element_type=f32)
         out_ref[:, lanes] = (mixed / total * gates[:, h : h + 1]).astype(bf16)
 
+    ring_step(2)
     attend(0)
-    ring_step(2)
     attend(1)
 
     for copy in c2:
@@ -404,8 +409,8 @@
         send(xa.at[p], xa.at[p], xa_send.at[d - 1], xa_recv.at[d - 1], plane_dev((p + d) % NP))
         for d in range(1, NP)
     ]
+    ring_step(3)
     attend(2)
-    ring_step(3)
     attend(3)
     attend(4)
     ring_step(4)
@@ -413,27 +418,38 @@
         attend(h)
     result_copy = pltpu.make_async_copy(out_ref, out_hbm, out_sem.at[0])
     result_copy.start()
-    for copy in near:
-        copy.wait_recv()
 
     for copy in ca:
         copy.wait_recv()
-    tokens = xa[...].astype(f32).reshape(NP * 8, 1024).astype(bf16)
-    parts = []
-    for n in range(2):
-        halves = []
-        for h in range(2):
-            total = jnp.zeros((NP * 8, CHUNK), f32)
-            for j in range(NZ // 2):
-                total = total + nt_dot(
-                    tokens[:, j * 128 : (j + 1) * 128],
-                    gathered[2 * j + h, n * CHUNK : (n + 1) * CHUNK, :],
-                )
-            halves.append(total)
-        parts.append(halves)
-    shift = NP * 8 - 4
-    unit_gate = parts[0][0] + roll(jnp.concatenate([parts[0][1], jnp.zeros((NP * 8, 32), f32)], axis=1), shift, 0)[:, :CHUNK]
-    unit_up = parts[1][0] + roll(jnp.concatenate([parts[1][1], jnp.zeros((NP * 8, 32), f32)], axis=1), shift, 0)[:, :CHUNK]
+
+    def product(away):
+        origin = (z + NZ + away) % NZ
+        lanes = pl.ds(pl.multiple_of(origin // 2 * 128, 128), 128)
+        tokens = xa[:, :, lanes].astype(f32).reshape(NP * 8, 128).astype(bf16)
+        return nt_dot(tokens, gathered[pl.ds(origin, 1), 0 : 2 * CHUNK, :][0])
+
+    same = product(0)
+    for away in (2, -2, 4, -4):
+        same = same + product(away)
+    for step, copy in near:
+        if step < 4:
+            copy.wait_recv()
+    other = product(1)
+    for away in (-1, 3, -3, 5, -5):
+        other = other + product(away)
+    same = same + product(6) + product(-6)
+    for step, copy in near:
+        if step == 4:
+            copy.wait_recv()
+    same = same + product(8)
+    other = other + product(7) + product(-7)
+    fill = jnp.zeros((NP * 8, 256 - 2 * CHUNK), f32)
+    same = jnp.concatenate([same, fill], axis=1)
+    other = jnp.concatenate([other, fill], axis=1)
+    swap = (iota((NP * 8, 256), 0) * 0 + z % 2) == 1
+    sums = jnp.where(swap, other, same) + roll(jnp.where(swap, same, other), NP * 8 - 4, 0)
+    unit_gate = sums[:, :CHUNK]
+    unit_up = roll(sums, 256 - CHUNK, 1)[:, :CHUNK]
     units = (unit_gate / (1.0 + jnp.exp(-unit_gate)) * unit_up).astype(bf16)
     low_rows = iota((NP * 8, 128), 0) % 8 < 4
     for j in range(NZ // 2):

time: 58.9 us -> 55.6 us (0.944)
  Pallas kernels: 55.8 us -> 52.5 us
    pallas_call x1, Pallas kernels: 55.8 us -> 52.5 us  [local(): pl.pallas_call(kernel, out_shape=(jax.ShapeDtypeStruct((TOK, HEADS * HD),...]
where the time goes in v4:
time: 55.6 us; the launch traced here: 55.5 us
  Pallas kernels  52.5 us (94%)
  local copies, waits for them, and re-layouts  2.28 us (4%)
  between operations  0.65 us (1%)
    pallas_call x1, Pallas kernels, local(): pl.pallas_call(kernel, out_shape=(jax.ShapeDtypeStruct((TOK, HEADS * HD),...  52.5 us
    unnamed x4, local copies, waits for them, and re-layouts  2.28 us

profile of v4, /device:TPU:1, one launch (start us, length us, event | category | flops | bytes accessed | tf_op | source)
XLA Modules:
  0.0 55.5 jit_solution(15100162931642414321)
XLA Ops:
  0.6 52.5 %shard_map.176 = (bf16[128,1024]{1,0:T(8,128)(2,1)}, bf16[3,2048]{1,0:T(4,128)(2,1)}) custom-call(s32[1,3]{1,0:T(1,128)} %lengths_ref.1, bf16[128,1024]{1,0:T(8,128)(2,1)} %q_hbm.1, bf16[8,128]{1,0:T(8,128)(2,1)} %bitcast.7, bf16[128,512]{1,0:T(8,128)(2,1)} %k_hbm.1, bf16[128,512]{1,0:T(8,128)(2,1)} %v_hbm.1, f32[1,128]{1,0:T(1,128)} %bitcast.8, ...), custom_call_target="tpu_custom_call" | custom-call | tf_op jit(solution)/shard_map/pallas_call | solution.py:522
  53.2 0.0 copy-start
  53.2 1.7 %copy.21 = bf16[128,1024]{1,0:T(8,128)(2,1)} copy(bf16[128,1024]{1,0:T(8,128)(2,1)} %get-tuple-element.4) | data formatting | bytes 524288
  54.9 0.0 copy-done
  54.9 0.6 %copy.22 = bf16[3,2048]{1,0:T(4,128)(2,1)} copy(bf16[3,2048]{1,0:T(4,128)(2,1)S(1)} %copy-done) | data formatting | bytes 24576
Async XLA Ops:
  53.2 1.7 %copy-start = (bf16[3,2048]{1,0:T(4,128)(2,1)S(1)}, bf16[3,2048]{1,0:T(4,128)(2,1)}, u32[]{:S(2)}) copy-start(bf16[3,2048]{1,0:T(4,128)(2,1)} %get-tuple-element.5) | copy-start | bytes 36868

commit v5 on v4

--- a/solution.py
+++ b/solution.py
@@ -152,6 +152,15 @@
     def z_dev(i):
         return {"z": i % NZ}
 
+    barrier = pltpu.get_barrier_semaphore()
+    mesh_id = pl.DeviceIdType.MESH
+    for d in range(1, NT):
+        pl.semaphore_signal(barrier, inc=1, device_id=tp_dev((t + d) % NT), device_id_type=mesh_id)
+    for d in range(1, NP):
+        pl.semaphore_signal(barrier, inc=1, device_id=plane_dev((p + d) % NP), device_id_type=mesh_id)
+    for d in (1, 2, NZ - 2, NZ - 1):
+        pl.semaphore_signal(barrier, inc=1, device_id=z_dev(z + d), device_id_type=mesh_id)
+
     loads = {}
     for n, (name, src, dst) in enumerate(
         (
@@ -179,15 +188,6 @@
     def arrive(*wanted):
         for name in wanted:
             loads[name].wait()
-
-    barrier = pltpu.get_barrier_semaphore()
-    mesh_id = pl.DeviceIdType.MESH
-    for d in range(1, NT):
-        pl.semaphore_signal(barrier, inc=1, device_id=tp_dev((t + d) % NT), device_id_type=mesh_id)
-    for d in range(1, NP):
-        pl.semaphore_signal(barrier, inc=1, device_id=plane_dev((p + d) % NP), device_id_type=mesh_id)
-    for d in (1, 2, NZ - 2, NZ - 1):
-        pl.semaphore_signal(barrier, inc=1, device_id=z_dev(z + d), device_id_type=mesh_id)
 
     started = []
 

time: 55.6 us -> 55.7 us (level)
  no operation moved by 1% of the time
where the time goes in v5:
time: 55.7 us; the launch traced here: 55.5 us
  Pallas kernels  52.6 us (94%)
  local copies, waits for them, and re-layouts  2.28 us (4%)
  between operations  0.65 us (1%)
    pallas_call x1, Pallas kernels, local(): pl.pallas_call(kernel, out_shape=(jax.ShapeDtypeStruct((TOK, HEADS * HD),...  52.6 us
    unnamed x4, local copies, waits for them, and re-layouts  2.28 us

profile of v5, /device:TPU:1, one launch (start us, length us, event | category | flops | bytes accessed | tf_op | source)
XLA Modules:
  0.0 55.5 jit_solution(10284382489469574212)
XLA Ops:
  0.6 52.6 %shard_map.176 = (bf16[128,1024]{1,0:T(8,128)(2,1)}, bf16[3,2048]{1,0:T(4,128)(2,1)}) custom-call(s32[1,3]{1,0:T(1,128)} %lengths_ref.1, bf16[128,1024]{1,0:T(8,128)(2,1)} %q_hbm.1, bf16[8,128]{1,0:T(8,128)(2,1)} %bitcast.7, bf16[128,512]{1,0:T(8,128)(2,1)} %k_hbm.1, bf16[128,512]{1,0:T(8,128)(2,1)} %v_hbm.1, f32[1,128]{1,0:T(1,128)} %bitcast.8, ...), custom_call_target="tpu_custom_call" | custom-call | tf_op jit(solution)/shard_map/pallas_call | solution.py:522
  53.2 0.0 copy-start
  53.2 1.7 %copy.21 = bf16[128,1024]{1,0:T(8,128)(2,1)} copy(bf16[128,1024]{1,0:T(8,128)(2,1)} %get-tuple-element.4) | data formatting | bytes 524288
  54.9 0.0 copy-done
  54.9 0.6 %copy.22 = bf16[3,2048]{1,0:T(4,128)(2,1)} copy(bf16[3,2048]{1,0:T(4,128)(2,1)S(1)} %copy-done) | data formatting | bytes 24576
Async XLA Ops:
  53.2 1.7 %copy-start = (bf16[3,2048]{1,0:T(4,128)(2,1)S(1)}, bf16[3,2048]{1,0:T(4,128)(2,1)}, u32[]{:S(2)}) copy-start(bf16[3,2048]{1,0:T(4,128)(2,1)} %get-tuple-element.5) | copy-start | bytes 36868
